TPU v7x, 512 devices: a whole 4x8x8 slice. The times are simulated.
512 devices in a mesh: wide: 32 (over y, x_hi, core), pair: 16 (over x_lo, z).
Axes of the slice: x: 4 (x_hi: 2, x_lo: 2; x = x_hi * 2 + x_lo), y: 8, z: 8, core: 2. Of those that a mesh axis runs over, the one named last changes fastest.
Arguments:
- rhs: bfloat16 [524288, 512], P(('wide', 'pair')), may hold values from -6 to 6
- coords: bfloat16 [1024, 2, 512], P(('wide', 'pair')), may hold values from 0 to 1
- near_index: int32 [1024, 3], P(('wide', 'pair')), may hold values from -2 to 2, as said below
- project_basis: bfloat16 [1024, 512, 192], P(('wide', 'pair')), may hold values from -0.25 to 0.25
- expand_basis: bfloat16 [1024, 512, 192], P(('wide', 'pair')), may hold values from -0.4375 to 0.4375
- transfer: bfloat16 [512, 5, 2, 192, 192], P(('wide', 'pair')), may hold values from -0.3125 to 0.3125
- level_perm: int32 [5, 192], replicated, may hold values from 0 to 191, each once within a row
Outputs:
- applied: bfloat16 [524288, 512], P(('wide', 'pair'))
Inputs may be any that keep to these rules, and one draw needn't show every extreme that they name: `near_index`: each row holds 3 different offsets. `level_perm`: each row is a permutation of 0 to 191.
All inputs are finite; a program needn't handle non-finite values.
Results may differ from a plain program's by a relative error of at most 0.0095.
Values may be sent and summed in bfloat16 or wider, within the bound.
No kernel may reach another device: no remote copies, remote signals or barrier semaphores. Data moves between devices by JAX's collectives and lax.ppermute only.
A program may use at most 64 MiB of HBM per device.

v0:
```python
import math

import jax
import jax.numpy as jnp
from jax import lax
from jax.sharding import PartitionSpec as P

NB = 3
LW = 3
LP = 2


softening = 0.0004


def with_halo(x, sides, width):
    edges = {}
    for axis, dim in sides:
        devices, length = (lax.axis_size(axis), x.shape[dim])
        up = [(i, (i + 1) % devices) for i in range(devices - 1)]
        last = lax.slice_in_dim(x, length - width, length, axis=dim)
        initial = lax.slice_in_dim(x, 0, width, axis=dim)
        edges[dim] = (
            lax.ppermute(last, axis, up),
            lax.ppermute(initial, axis, [(b, a) for a, b in up]),
        )
    done = []
    for _, dim in sides:
        low, high = edges[dim]
        around = [(width, width) if d in done else (0, 0) for d in range(x.ndim)]
        x = jnp.concatenate([jnp.pad(low, around), x, jnp.pad(high, around)], axis=dim)
        done.append(dim)
    return x


def from_partner(block, axis, bit):
    count = lax.axis_size(axis)
    route = []
    for low in range(count):
        high = low | 1 << bit
        if high != low and high < count:
            route += [(low, high), (high, low)]
    return lax.ppermute(block, axis, route)


def kernel_tile(target, source):
    delta_x = target[0][:, None] - source[0][None, :]
    delta_y = target[1][:, None] - source[1][None, :]
    factor = 0.25 / math.sqrt(target.shape[1])
    return (lax.rsqrt(delta_x * delta_x + delta_y * delta_y + softening) * factor).astype(
        jnp.bfloat16
    )


def on_device(rhs, coords, near_index, project_basis, expand_basis, transfer, level_perm):
    own_leaves = coords.shape[0]
    leaf_rows = coords.shape[2]
    columns = rhs.shape[1]
    leaves = rhs.reshape(own_leaves, leaf_rows, columns)
    points = coords.astype(jnp.float32)
    padded_rhs, padded_points = (
        with_halo(leaves, ((("wide", "pair"), 0),), 2),
        with_halo(coords, ((("wide", "pair"), 0),), 2),
    )
    gathered = []
    for target in range(own_leaves):
        summed = jnp.zeros((leaf_rows, columns), jnp.float32)
        for slot in range(NB):
            position = target + 2 + near_index[target, slot]
            source_rows = lax.dynamic_index_in_dim(padded_rhs, position, 0, keepdims=False)
            source_points = lax.dynamic_index_in_dim(
                padded_points, position, 0, keepdims=False
            ).astype(jnp.float32)
            tile = kernel_tile(points[target], source_points)
            summed = summed + jnp.dot(tile, source_rows, preferred_element_type=jnp.float32)
        gathered.append(summed)
    nearby = jnp.stack(gathered)
    projected = jnp.zeros((project_basis.shape[2], columns), jnp.float32)
    for target in range(own_leaves):
        projected = projected + jnp.einsum(
            "lr,lc->rc", project_basis[target], leaves[target], preferred_element_type=jnp.float32
        )
    projected = projected.astype(jnp.bfloat16)
    for level_bit in range(LW):
        partner_rows = from_partner(projected, "wide", level_bit)[level_perm[level_bit]]
        updated = jnp.dot(transfer[0, level_bit, 0], projected, preferred_element_type=jnp.float32)
        updated = updated + jnp.dot(
            transfer[0, level_bit, 1], partner_rows, preferred_element_type=jnp.float32
        )
        projected = updated.astype(jnp.bfloat16)
    for level_bit in range(LP):
        partner_rows = from_partner(projected, "pair", level_bit)[level_perm[LW + level_bit]]
        updated = jnp.dot(
            transfer[0, LW + level_bit, 0], projected, preferred_element_type=jnp.float32
        )
        updated = updated + jnp.dot(
            transfer[0, LW + level_bit, 1], partner_rows, preferred_element_type=jnp.float32
        )
        projected = updated.astype(jnp.bfloat16)
    distant = jnp.einsum("nlr,rc->nlc", expand_basis, projected, preferred_element_type=jnp.float32)
    return (nearby + distant).reshape(own_leaves * leaf_rows, columns).astype(jnp.bfloat16)


def solution(mesh):
    return jax.shard_map(
        on_device,
        mesh=mesh,
        in_specs=(
            P(("wide", "pair"), None),
            P(("wide", "pair"), None, None),
            P(("wide", "pair"), None),
            P(("wide", "pair"), None, None),
            P(("wide", "pair"), None, None),
            P(("wide", "pair"), None, None, None, None),
            P(),
        ),
        out_specs=P(("wide", "pair"), None),
        check_vma=False,
    )
```

profile of v0, /device:TPU:1, one launch (start us, length us, event | category | flops | bytes accessed | tf_op | source)
XLA Modules:
  0.0 97.6 jit_solution(16711656396360844590)
XLA Ops:
  0.0 5.0 %collective-permute-start = (bf16[2,2,512]{2,1,0:T(2,128)(2,1)}, bf16[2,2,512]{2,1,0:T(2,128)(2,1)S(1)}, u32[]{:S(2)}, u32[]{:S(2)}) collective-permute-start(bf16[2,2,512]{2,1,0:T(2,128)(2,1)} %param.8), channel_id=1, source_target_pairs={{0,1},{1,2},{2,3},{3,4},{4,5},{5,6},{6,7},{7,8},{8,9},{9,10},{10,1... | collective-permute-start | bytes 12296 | tf_op jit(solution)/shard_map/ppermute | solution.py:24
  5.0 10.1 %collective-permute-start.1 = (bf16[2,2,512]{2,1,0:T(2,128)(2,1)}, bf16[2,2,512]{2,1,0:T(2,128)(2,1)S(1)}, u32[]{:S(2)}, u32[]{:S(2)}) collective-permute-start(bf16[2,2,512]{2,1,0:T(2,128)(2,1)} %param.8), channel_id=1, source_target_pairs={{1,0},{2,1},{3,2},{4,3},{5,4},{6,5},{7,6},{8,7},{9,8},{10,9},{11,1... | collective-permute-start | bytes 12296 | tf_op jit(solution)/shard_map/ppermute | solution.py:25
  15.1 1.9 %collective-permute-start.2 = (bf16[2,512,512]{2,1,0:T(8,128)(2,1)}, bf16[2,512,512]{2,1,0:T(8,128)(2,1)S(1)}, u32[]{:S(2)}, u32[]{:S(2)}) collective-permute-start(bf16[2,512,512]{2,1,0:T(8,128)(2,1)} %bitcast.125), channel_id=1, source_target_pairs={{0,1},{1,2},{2,3},{3,4},{4,5},{5,6},{6,7},{7,8},{8,9},{9,10},{10,1... | collective-permute-start | bytes 3145736 | tf_op jit(solution)/shard_map/ppermute | solution.py:24
  17.0 5.8 %collective-permute-start.3 = (bf16[2,512,512]{2,1,0:T(8,128)(2,1)}, bf16[2,512,512]{2,1,0:T(8,128)(2,1)}, u32[]{:S(2)}, u32[]{:S(2)}) collective-permute-start(bf16[2,512,512]{2,1,0:T(8,128)(2,1)} %bitcast.126), channel_id=1, source_target_pairs={{1,0},{2,1},{3,2},{4,3},{5,4},{6,5},{7,6},{8,7},{9,8},{10,9},{11,1... | collective-permute-start | bytes 3145736 | tf_op jit(solution)/shard_map/ppermute | solution.py:25
  22.7 1.4 %fusion.23 = f32[192,512]{1,0:T(8,128)S(1)} fusion(bf16[1024,512]{1,0:T(8,128)(2,1)} %param.7, bf16[2,512,192]{1,2,0:T(8,128)(2,1)} %param.10), kind=kOutput, calls=%fused_computation.44 | convolution fusion | flops 100663296 | bytes 1114112 | tf_op jit(solution)/shard_map/lr,lc->rc/dot_general | solution.py:80
  24.2 1.4 %fusion.10 = bf16[192,512]{1,0:T(8,128)(2,1)S(1)} fusion(f32[192,512]{1,0:T(8,128)S(1)} %fusion.23, bf16[1024,512]{1,0:T(8,128)(2,1)} %param.7, bf16[2,512,192]{1,2,0:T(8,128)(2,1)} %param.10), kind=kOutput, calls=%fused_computation.25 | convolution fusion | flops 100859904 | bytes 1310720 | tf_op jit(solution)/shard_map/lr,lc->rc/dot_general | solution.py:80
  25.6 1.9 %collective-permute-start.4 = (bf16[192,512]{1,0:T(8,128)(2,1)S(1)}, bf16[192,512]{1,0:T(8,128)(2,1)S(1)}, u32[]{:S(2)}, u32[]{:S(2)}) collective-permute-start(bf16[192,512]{1,0:T(8,128)(2,1)S(1)} %fusion.10), channel_id=1, source_target_pairs={{0,16},{16,0},{32,48},{48,32},{64,80},{80,64},{96,112},{112,96},{1... | collective-permute-start | bytes 589832 | tf_op jit(solution)/shard_map/ppermute | solution.py:43
  28.3 1.6 %fusion.129 = (s32[1,1]{1,0:T(1,128)}, s32[1,1]{1,0:T(1,128)}, s32[1,1]{1,0:T(1,128)}, s32[1,1]{1,0:T(1,128)}, s32[1,1]{1,0:T(1,128)}, /*index=5*/s32[1,1]{1,0:T(1,128)}) fusion(s32[2,3]{1,0:T(2,128)} %param.9), kind=kLoop, calls=%fused_computation.167 | loop fusion | bytes 48 | tf_op jit(solution)/shard_map/slice | solution.py:69
  40.5 1.1 %fusion.5 = bf16[512,192]{0,1:T(8,128)(2,1)S(1)} fusion(f32[512,192]{0,1:T(8,128)S(1)} %fusion.85, bf16[192,512]{1,0:T(8,128)(2,1)S(1)} %gather_fusion, bf16[1,5,2,192,192]{4,3,2,1,0:T(8,128)(2,1)} %param.12), kind=kOutput, calls=%fused_computation.20 | convolution fusion | flops 37945344 | bytes 884736 | tf_op jit(solution)/shard_map/dot_general | solution.py:87
  41.6 4.4 %collective-permute-start.5 = (bf16[192,512]{1,0:T(8,128)(2,1)S(1)}, bf16[192,512]{1,0:T(8,128)(2,1)S(1)}, u32[]{:S(2)}, u32[]{:S(2)}) collective-permute-start(bf16[192,512]{1,0:T(8,128)(2,1)S(1)} %bitcast.128), channel_id=1, source_target_pairs={{0,32},{32,0},{16,48},{48,16},{64,96},{96,64},{80,112},{112,80},{1... | collective-permute-start | bytes 589832 | tf_op jit(solution)/shard_map/ppermute | solution.py:43
  46.0 1.1 %fusion.82 = f32[512,192]{0,1:T(8,128)S(1)} fusion(bf16[512,192]{0,1:T(8,128)(2,1)S(1)} %fusion.5, bf16[1,5,2,192,192]{4,3,2,1,0:T(8,128)(2,1)} %param.12), kind=kOutput, calls=%fused_computation.102 | convolution fusion | flops 37748736 | bytes 688128 | tf_op jit(solution)/shard_map/dot_general | solution.py:86
  47.1 3.9 %collective-permute-done.5 = bf16[192,512]{1,0:T(8,128)(2,1)S(1)} collective-permute-done((bf16[192,512]{1,0:T(8,128)(2,1)S(1)}, bf16[192,512]{1,0:T(8,128)(2,1)S(1)}, u32[]{:S(2)}, u32[]{:S(2)}) %collective-permute-start.5) | collective-permute-done | bytes 196640 | tf_op jit(solution)/shard_map/ppermute | solution.py:43
  52.0 1.1 %fusion.6 = bf16[512,192]{0,1:T(8,128)(2,1)S(1)} fusion(f32[512,192]{0,1:T(8,128)S(1)} %fusion.82, bf16[192,512]{1,0:T(8,128)(2,1)S(1)} %gather_fusion.1, bf16[1,5,2,192,192]{4,3,2,1,0:T(8,128)(2,1)} %param.12), kind=kOutput, calls=%fused_computation.21 | convolution fusion | flops 37945344 | bytes 884736 | tf_op jit(solution)/shard_map/dot_general | solution.py:87
  53.1 6.9 %collective-permute-start.6 = (bf16[192,512]{1,0:T(8,128)(2,1)S(1)}, bf16[192,512]{1,0:T(8,128)(2,1)S(1)}, u32[]{:S(2)}, u32[]{:S(2)}) collective-permute-start(bf16[192,512]{1,0:T(8,128)(2,1)S(1)} %bitcast.129), channel_id=1, source_target_pairs={{0,64},{64,0},{16,80},{80,16},{32,96},{96,32},{48,112},{112,48},{1... | collective-permute-start | bytes 589832 | tf_op jit(solution)/shard_map/ppermute | solution.py:43
  61.1 3.4 %collective-permute-done.6 = bf16[192,512]{1,0:T(8,128)(2,1)S(1)} collective-permute-done((bf16[192,512]{1,0:T(8,128)(2,1)S(1)}, bf16[192,512]{1,0:T(8,128)(2,1)S(1)}, u32[]{:S(2)}, u32[]{:S(2)}) %collective-permute-start.6) | collective-permute-done | bytes 196640 | tf_op jit(solution)/shard_map/ppermute | solution.py:43
  65.5 1.2 %fusion.7 = bf16[512,192]{0,1:T(8,128)(2,1)S(1)} fusion(f32[512,192]{0,1:T(8,128)S(1)} %fusion.79, bf16[192,512]{1,0:T(8,128)(2,1)S(1)} %gather_fusion.2, bf16[1,5,2,192,192]{4,3,2,1,0:T(8,128)(2,1)} %param.12), kind=kOutput, calls=%fused_computation.22 | convolution fusion | flops 37945344 | bytes 884736 | tf_op jit(solution)/shard_map/dot_general | solution.py:87
  66.7 1.9 %collective-permute-start.7 = (bf16[192,512]{1,0:T(8,128)(2,1)S(1)}, bf16[192,512]{1,0:T(8,128)(2,1)S(1)}, u32[]{:S(2)}, u32[]{:S(2)}) collective-permute-start(bf16[192,512]{1,0:T(8,128)(2,1)S(1)} %bitcast.130), channel_id=1, source_target_pairs={{0,1},{1,0},{2,3},{3,2},{4,5},{5,4},{6,7},{7,6},{8,9},{9,8},{10,11... | collective-permute-start | bytes 589832 | tf_op jit(solution)/shard_map/ppermute | solution.py:43
  69.7 3.9 %collective-permute-done.7 = bf16[192,512]{1,0:T(8,128)(2,1)S(1)} collective-permute-done((bf16[192,512]{1,0:T(8,128)(2,1)S(1)}, bf16[192,512]{1,0:T(8,128)(2,1)S(1)}, u32[]{:S(2)}, u32[]{:S(2)}) %collective-permute-start.7) | collective-permute-done | bytes 196640 | tf_op jit(solution)/shard_map/ppermute | solution.py:43
  74.6 1.1 %fusion.8 = bf16[512,192]{0,1:T(8,128)(2,1)S(1)} fusion(f32[512,192]{0,1:T(8,128)S(1)} %fusion.76, bf16[192,512]{1,0:T(8,128)(2,1)S(1)} %gather_fusion.3, bf16[1,5,2,192,192]{4,3,2,1,0:T(8,128)(2,1)} %param.12), kind=kOutput, calls=%fused_computation.23 | convolution fusion | flops 37945344 | bytes 884736 | tf_op jit(solution)/shard_map/dot_general | solution.py:96
  75.7 1.9 %collective-permute-start.8 = (bf16[192,512]{1,0:T(8,128)(2,1)S(1)}, bf16[192,512]{1,0:T(8,128)(2,1)S(1)}, u32[]{:S(2)}, u32[]{:S(2)}) collective-permute-start(bf16[192,512]{1,0:T(8,128)(2,1)S(1)} %bitcast.131), channel_id=1, source_target_pairs={{0,2},{2,0},{1,3},{3,1},{4,6},{6,4},{5,7},{7,5},{8,10},{10,8},{9,1... | collective-permute-start | bytes 589832 | tf_op jit(solution)/shard_map/ppermute | solution.py:43
  77.6 1.1 %fusion.73 = f32[512,192]{0,1:T(8,128)S(1)} fusion(bf16[512,192]{0,1:T(8,128)(2,1)S(1)} %fusion.8, bf16[1,5,2,192,192]{4,3,2,1,0:T(8,128)(2,1)} %param.12), kind=kOutput, calls=%fused_computation.93 | convolution fusion | flops 37748736 | bytes 688128 | tf_op jit(solution)/shard_map/dot_general | solution.py:93
  78.7 10.5 %collective-permute-done.8 = bf16[192,512]{1,0:T(8,128)(2,1)S(1)} collective-permute-done((bf16[192,512]{1,0:T(8,128)(2,1)S(1)}, bf16[192,512]{1,0:T(8,128)(2,1)S(1)}, u32[]{:S(2)}, u32[]{:S(2)}) %collective-permute-start.8) | collective-permute-done | bytes 196640 | tf_op jit(solution)/shard_map/ppermute | solution.py:43
  90.2 1.4 %pad_maximum_fusion = bf16[6,512,512]{2,1,0:T(8,128)(2,1)S(1)} fusion(bf16[2,512,512]{2,1,0:T(8,128)(2,1)} %collective-permute-done.3, bf16[2,512,512]{2,1,0:T(8,128)(2,1)S(1)} %bitcast.127, bf16[2,512,512]{2,1,0:T(8,128)(2,1)S(1)} %collective-permute-done.2), kind=kLoop, calls=%fused_computation.5 | loop fusion | flops 3145728 | bytes 6291456 | tf_op jit(solution)/shard_map/concatenate | solution.py:31
  95.1 2.5 %fusion = bf16[2,512,512]{2,1,0:T(8,128)(2,1)} fusion(f32[1,512,512]{2,1,0:T(8,128)S(1)} %fusion.2, f32[1,512,512]{2,1,0:T(8,128)S(1)} %fusion.4, bf16[2,512,192]{1,2,0:T(8,128)(2,1)S(1)} %copy-done, f32[512,192]{0,1:T(8,128)S(1)} %fusion.73, bf16[192,512]{1,0:T(8,128)(2,1)S(1)} %gather_fusion.4, bf16[1,5,2,192,192]{4,3,2,1,0:T(8,128)(2,1)} %param.12), kind=kOutput, calls=%fused_computation.7 | convolution fusion | flops 240844800 | bytes 4227072 | tf_op jit(solution)/shard_map/nlr,rc->nlc/dot_general | solution.py:100
  (39 shorter events, 13.5 us)
Async XLA Ops:
  0.0 95.1 %copy-start = (bf16[2,512,192]{1,2,0:T(8,128)(2,1)S(1)}, bf16[2,512,192]{1,2,0:T(8,128)(2,1)}, u32[]{:S(2)}) copy-start(bf16[2,512,192]{1,2,0:T(8,128)(2,1)} %param.11) | copy-start | bytes 1179652
  0.0 39.4 %copy-start.2 = (bf16[2,2,512]{2,1,0:T(2,128)(2,1)S(1)}, bf16[2,2,512]{2,1,0:T(2,128)(2,1)}, u32[]{:S(2)}) copy-start(bf16[2,2,512]{2,1,0:T(2,128)(2,1)} %param.8) | copy-start | bytes 12292
  0.0 39.4 %collective-permute-start = (bf16[2,2,512]{2,1,0:T(2,128)(2,1)}, bf16[2,2,512]{2,1,0:T(2,128)(2,1)S(1)}, u32[]{:S(2)}, u32[]{:S(2)}) collective-permute-start(bf16[2,2,512]{2,1,0:T(2,128)(2,1)} %param.8), channel_id=1, source_target_pairs={{0,1},{1,2},{2,3},{3,4},{4,5},{5,6},{6,7},{7,8},{8,9},{9,10},{10,1... | collective-permute-start | bytes 12296 | tf_op jit(solution)/shard_map/ppermute | solution.py:24
  5.0 34.5 %collective-permute-start.1 = (bf16[2,2,512]{2,1,0:T(2,128)(2,1)}, bf16[2,2,512]{2,1,0:T(2,128)(2,1)S(1)}, u32[]{:S(2)}, u32[]{:S(2)}) collective-permute-start(bf16[2,2,512]{2,1,0:T(2,128)(2,1)} %param.8), channel_id=1, source_target_pairs={{1,0},{2,1},{3,2},{4,3},{5,4},{6,5},{7,6},{8,7},{9,8},{10,9},{11,1... | collective-permute-start | bytes 12296 | tf_op jit(solution)/shard_map/ppermute | solution.py:25
  15.1 75.1 %collective-permute-start.2 = (bf16[2,512,512]{2,1,0:T(8,128)(2,1)}, bf16[2,512,512]{2,1,0:T(8,128)(2,1)S(1)}, u32[]{:S(2)}, u32[]{:S(2)}) collective-permute-start(bf16[2,512,512]{2,1,0:T(8,128)(2,1)} %bitcast.125), channel_id=1, source_target_pairs={{0,1},{1,2},{2,3},{3,4},{4,5},{5,6},{6,7},{7,8},{8,9},{9,10},{10,1... | collective-permute-start | bytes 3145736 | tf_op jit(solution)/shard_map/ppermute | solution.py:24
  17.0 73.2 %collective-permute-start.3 = (bf16[2,512,512]{2,1,0:T(8,128)(2,1)}, bf16[2,512,512]{2,1,0:T(8,128)(2,1)}, u32[]{:S(2)}, u32[]{:S(2)}) collective-permute-start(bf16[2,512,512]{2,1,0:T(8,128)(2,1)} %bitcast.126), channel_id=1, source_target_pairs={{1,0},{2,1},{3,2},{4,3},{5,4},{6,5},{7,6},{8,7},{9,8},{10,9},{11,1... | collective-permute-start | bytes 3145736 | tf_op jit(solution)/shard_map/ppermute | solution.py:25
  25.6 14.0 %collective-permute-start.4 = (bf16[192,512]{1,0:T(8,128)(2,1)S(1)}, bf16[192,512]{1,0:T(8,128)(2,1)S(1)}, u32[]{:S(2)}, u32[]{:S(2)}) collective-permute-start(bf16[192,512]{1,0:T(8,128)(2,1)S(1)} %fusion.10), channel_id=1, source_target_pairs={{0,16},{16,0},{32,48},{48,32},{64,80},{80,64},{96,112},{112,96},{1... | collective-permute-start | bytes 589832 | tf_op jit(solution)/shard_map/ppermute | solution.py:43
  41.6 9.4 %collective-permute-start.5 = (bf16[192,512]{1,0:T(8,128)(2,1)S(1)}, bf16[192,512]{1,0:T(8,128)(2,1)S(1)}, u32[]{:S(2)}, u32[]{:S(2)}) collective-permute-start(bf16[192,512]{1,0:T(8,128)(2,1)S(1)} %bitcast.128), channel_id=1, source_target_pairs={{0,32},{32,0},{16,48},{48,16},{64,96},{96,64},{80,112},{112,80},{1... | collective-permute-start | bytes 589832 | tf_op jit(solution)/shard_map/ppermute | solution.py:43
  53.1 11.4 %collective-permute-start.6 = (bf16[192,512]{1,0:T(8,128)(2,1)S(1)}, bf16[192,512]{1,0:T(8,128)(2,1)S(1)}, u32[]{:S(2)}, u32[]{:S(2)}) collective-permute-start(bf16[192,512]{1,0:T(8,128)(2,1)S(1)} %bitcast.129), channel_id=1, source_target_pairs={{0,64},{64,0},{16,80},{80,16},{32,96},{96,32},{48,112},{112,48},{1... | collective-permute-start | bytes 589832 | tf_op jit(solution)/shard_map/ppermute | solution.py:43
  65.5 24.7 %copy-start.1 = (bf16[1024,512]{1,0:T(8,128)(2,1)S(1)}, bf16[1024,512]{1,0:T(8,128)(2,1)}, u32[]{:S(2)}) copy-start(bf16[1024,512]{1,0:T(8,128)(2,1)} %param.7) | copy-start | bytes 3145732
  66.7 6.9 %collective-permute-start.7 = (bf16[192,512]{1,0:T(8,128)(2,1)S(1)}, bf16[192,512]{1,0:T(8,128)(2,1)S(1)}, u32[]{:S(2)}, u32[]{:S(2)}) collective-permute-start(bf16[192,512]{1,0:T(8,128)(2,1)S(1)} %bitcast.130), channel_id=1, source_target_pairs={{0,1},{1,0},{2,3},{3,2},{4,5},{5,4},{6,7},{7,6},{8,9},{9,8},{10,11... | collective-permute-start | bytes 589832 | tf_op jit(solution)/shard_map/ppermute | solution.py:43
  75.7 13.5 %collective-permute-start.8 = (bf16[192,512]{1,0:T(8,128)(2,1)S(1)}, bf16[192,512]{1,0:T(8,128)(2,1)S(1)}, u32[]{:S(2)}, u32[]{:S(2)}) collective-permute-start(bf16[192,512]{1,0:T(8,128)(2,1)S(1)} %bitcast.131), channel_id=1, source_target_pairs={{0,2},{2,0},{1,3},{3,1},{4,6},{6,4},{5,7},{7,5},{8,10},{10,8},{9,1... | collective-permute-start | bytes 589832 | tf_op jit(solution)/shard_map/ppermute | solution.py:43
where the time goes:
time: 98.5 us; the launch traced here: 97.6 us
  starting transfers between devices  39.7 us (40%)
  waiting for transfers between devices  21.7 us (22%)
  matrix products  18.6 us (19%)
  between operations  7.81 us (8%)
  local copies, waits for them, and re-layouts  7.41 us (8%)
  other arithmetic  2.38 us (2%)
    ppermute x5, waiting for transfers between devices, from_partner(): return lax.ppermute(block, axis, route)  21.6 us
    ppermute x5, starting transfers between devices, from_partner(): return lax.ppermute(block, axis, route)  17 us
    ppermute x2, starting transfers between devices, with_halo(): lax.ppermute(initial, axis, [(b, a) for a, b in up])  15.8 us
    ppermute x2, starting transfers between devices, with_halo(): lax.ppermute(last, axis, up)  6.87 us
    dot_general x6, matrix products, on_device(): jnp.dot(tile, source_rows, preferred_element_type=jnp.float32)  3.41 us
    dot_general x3, matrix products, on_device(): jnp.dot(transfer[0, level_bit, 1], partner_rows, preferred_element_type=j...  3.36 us
    dot_general x3, matrix products, on_device(): jnp.dot(transfer[0, level_bit, 0], projected, preferred_element_type=jnp....  3.27 us
    gather x3, local copies, waits for them, and re-layouts, on_device(): from_partner(projected, 'wide', level_bit)[level_perm[level_bit]]  3 us
  transfers between devices with their start and end apart: 9, of which 4 were waited for; matrix products, arithmetic and copies ran while one was open for 22% of the time, Pallas kernels for 0%

commit v1 on v0

v1 whole, which is shorter than its diff:
```python
import math

import jax
import jax.numpy as jnp
from jax import lax
from jax.experimental import pallas as pl
from jax.experimental.pallas import tpu as pltpu
from jax.sharding import PartitionSpec as P

LW = 3
LP = 2
LEVELS = LW + LP
LEAF = 512
RANK = 192
COLS = 512
ROWS = 1024
PACK = ROWS + 16
SOFT = 0.0004
FACTOR = 0.25 / math.sqrt(LEAF)
F32 = jnp.float32
BF16 = jnp.bfloat16
VMEM = pl.BlockSpec(memory_space=pltpu.VMEM)
SMEM = pl.BlockSpec(memory_space=pltpu.SMEM)


def params():
    return pltpu.CompilerParams(vmem_limit_bytes=40 << 20)


def project_kernel(x_ref, basis_ref, coords_ref, s_ref, pack_ref):
    total = jnp.dot(basis_ref[0], x_ref[:LEAF, :], preferred_element_type=F32)
    total = total + jnp.dot(basis_ref[1], x_ref[LEAF:, :], preferred_element_type=F32)
    s_ref[...] = total.astype(BF16)
    pack_ref[:ROWS, :] = x_ref[...]
    pack_ref[ROWS:, :] = jnp.concatenate(
        [coords_ref[...], jnp.zeros((12, COLS), BF16)], axis=0
    )


def project(x, basis_t, coords4):
    return pl.pallas_call(
        project_kernel,
        out_shape=(
            jax.ShapeDtypeStruct((RANK, COLS), BF16),
            jax.ShapeDtypeStruct((PACK, COLS), BF16),
        ),
        in_specs=[VMEM, VMEM, VMEM],
        out_specs=(VMEM, VMEM),
        compiler_params=params(),
        name="project",
    )(x, basis_t, coords4)


def prepare_kernel(transfer_ref, perm_ref, expand_ref, t_ref, e_ref):
    k = lax.broadcasted_iota(jnp.int32, (RANK, RANK), 0)
    for level in range(LEVELS):
        t_ref[level, 0] = transfer_ref[level, 0]
        picked = jnp.where(k == perm_ref[level : level + 1, :], 1.0, 0.0).astype(BF16)
        t_ref[level, 1] = lax.dot_general(
            transfer_ref[level, 1], picked, (((1,), (1,)), ((), ())), preferred_element_type=F32
        ).astype(BF16)
    for leaf in range(2):
        e_ref[leaf * LEAF : (leaf + 1) * LEAF, :] = expand_ref[leaf].T


def prepare(transfer, perm, expand_t):
    return pl.pallas_call(
        prepare_kernel,
        out_shape=(
            jax.ShapeDtypeStruct((LEVELS, 2, RANK, RANK), BF16),
            jax.ShapeDtypeStruct((ROWS, RANK), BF16),
        ),
        in_specs=[VMEM, VMEM, VMEM],
        out_specs=(VMEM, VMEM),
        compiler_params=params(),
        name="prepare",
    )(transfer, perm, expand_t)


def level_kernel(t_ref, own_ref, other_ref, s_ref):
    total = jnp.dot(t_ref[0, 0], own_ref[...], preferred_element_type=F32)
    total = total + jnp.dot(t_ref[0, 1], other_ref[...], preferred_element_type=F32)
    s_ref[...] = total.astype(BF16)


def level_step(level, t, own, other):
    return pl.pallas_call(
        level_kernel,
        grid=(1,),
        out_shape=jax.ShapeDtypeStruct((RANK, COLS), BF16),
        in_specs=[
            pl.BlockSpec((1, 2, RANK, RANK), lambda i: (level, 0, 0, 0)),
            pl.BlockSpec((RANK, COLS), lambda i: (0, 0)),
            pl.BlockSpec((RANK, COLS), lambda i: (0, 0)),
        ],
        out_specs=pl.BlockSpec((RANK, COLS), lambda i: (0, 0)),
        compiler_params=params(),
        name=f"level{level}",
    )(t, own, other)


def near_kernel(index_ref, own_ref, low_ref, high_ref, near_ref):
    sides = (low_ref, own_ref, high_ref)
    scale = 1.0 / FACTOR
    points = own_ref[ROWS : ROWS + 8, :].astype(F32) * scale
    columns = points.T
    rows = [side[ROWS : ROWS + 8, :].astype(F32) * scale for side in sides]
    for target in range(2):
        block = pl.ds(target * LEAF, LEAF)
        near_ref[block, :] = jnp.zeros((LEAF, COLS), F32)
        tx = columns[:, 2 * target : 2 * target + 1]
        ty = columns[:, 2 * target + 1 : 2 * target + 2]
        for offset in (0, 1, -1, 2, -2):
            side, leaf = divmod(target + offset + 2, 2)
            used = (
                (index_ref[target, 0] == offset)
                | (index_ref[target, 1] == offset)
                | (index_ref[target, 2] == offset)
            )

            @pl.when(used)
            def _(side=side, leaf=leaf, tx=tx, ty=ty, block=block):
                sx = rows[side][2 * leaf : 2 * leaf + 1, :]
                sy = rows[side][2 * leaf + 1 : 2 * leaf + 2, :]
                dx = tx - sx
                dy = ty - sy
                tile = lax.rsqrt(dx * dx + dy * dy + SOFT * scale * scale).astype(BF16)
                near_ref[block, :] += jnp.dot(
                    tile,
                    sides[side][leaf * LEAF : (leaf + 1) * LEAF, :],
                    preferred_element_type=F32,
                )


def near_field(index, own, low, high):
    return pl.pallas_call(
        near_kernel,
        out_shape=jax.ShapeDtypeStruct((ROWS, COLS), F32),
        in_specs=[SMEM, VMEM, VMEM, VMEM],
        out_specs=VMEM,
        compiler_params=params(),
        name="near",
    )(index, own, low, high)


def final_kernel(t_ref, own_ref, other_ref, e_ref, near_ref, out_ref, s_ref):
    @pl.when(pl.program_id(0) == 0)
    def _():
        total = jnp.dot(t_ref[0, 0], own_ref[...], preferred_element_type=F32)
        total = total + jnp.dot(t_ref[0, 1], other_ref[...], preferred_element_type=F32)
        s_ref[...] = total.astype(BF16)

    distant = jnp.dot(e_ref[...], s_ref[...], preferred_element_type=F32)
    out_ref[...] = (near_ref[...] + distant).astype(BF16)


def final_step(t, own, other, e, near):
    block = 256
    return pl.pallas_call(
        final_kernel,
        grid=(ROWS // block,),
        out_shape=jax.ShapeDtypeStruct((ROWS, COLS), BF16),
        in_specs=[
            pl.BlockSpec((1, 2, RANK, RANK), lambda i: (LEVELS - 1, 0, 0, 0)),
            pl.BlockSpec((RANK, COLS), lambda i: (0, 0)),
            pl.BlockSpec((RANK, COLS), lambda i: (0, 0)),
            pl.BlockSpec((block, RANK), lambda i: (i, 0)),
            pl.BlockSpec((block, COLS), lambda i: (i, 0)),
        ],
        out_specs=pl.BlockSpec((block, COLS), lambda i: (i, 0)),
        scratch_shapes=[pltpu.VMEM((RANK, COLS), BF16)],
        compiler_params=params(),
        name="final",
    )(t, own, other, e, near)


def from_partner(block, axis, bit):
    count = lax.axis_size(axis)
    return lax.ppermute(block, axis, [(i, i ^ (1 << bit)) for i in range(count)])


def on_device(rhs, coords, near_index, project_basis, expand_basis, transfer, level_perm):
    axes = ("wide", "pair")
    devices = lax.axis_size("wide") * lax.axis_size("pair")
    up = [(i, i + 1) for i in range(devices - 1)]
    down = [(i + 1, i) for i in range(devices - 1)]
    s, pack = project(rhs, jnp.swapaxes(project_basis, 1, 2), coords.reshape(4, LEAF))
    partner = from_partner(s, "wide", 0)
    low = lax.ppermute(pack, axes, up)
    high = lax.ppermute(pack, axes, down)
    t, e = prepare(transfer[0], level_perm, jnp.swapaxes(expand_basis, 1, 2))
    for level in range(LEVELS - 1):
        s = level_step(level, t, s, partner)
        if level + 1 < LW:
            partner = from_partner(s, "wide", level + 1)
        else:
            partner = from_partner(s, "pair", level + 1 - LW)
    near = near_field(near_index, pack, low, high)
    return final_step(t, s, partner, e, near)


def solution(mesh):
    return jax.shard_map(
        on_device,
        mesh=mesh,
        in_specs=(
            P(("wide", "pair"), None),
            P(("wide", "pair"), None, None),
            P(("wide", "pair"), None),
            P(("wide", "pair"), None, None),
            P(("wide", "pair"), None, None),
            P(("wide", "pair"), None, None, None, None),
            P(),
        ),
        out_specs=P(("wide", "pair"), None),
        check_vma=False,
    )
```

time: 98.5 us -> 83.2 us (0.84)
  waiting for transfers between devices: 21.7 us -> 42.9 us
  matrix products: 18.6 us -> 0 us
  starting transfers between devices: 39.7 us -> 28.3 us
  Pallas kernels: 0 us -> 8.37 us
  between operations: 7.81 us -> 0.17 us
  local copies, waits for them, and re-layouts: 7.41 us -> 2.95 us
  other arithmetic: 2.38 us -> 0 us
    ppermute x9 -> x7, waiting for transfers between devices: 21.7 us -> 42.9 us  [the longest x5 42.9 us: from_partner(): return lax.ppermute(block, axis, [(i, i ^ 1 << bit) for i in range(count)])]
    dot_general x18 -> x0, matrix products: 18.6 us -> none  [the longest x6 3.41 us: on_device(): jnp.dot(tile, source_rows, preferred_element_type=jnp.float32)]
    ppermute x9 -> x7, starting transfers between devices: 39.7 us -> 28.3 us  [the longest x5 13.3 us: from_partner(): return lax.ppermute(block, axis, [(i, i ^ 1 << bit) for i in range(count)])]
    pallas_call x0 -> x8, Pallas kernels: none -> 8.37 us  [the longest x1 4.27 us: near_field(): pl.pallas_call(near_kernel, out_shape=jax.ShapeDtypeStruct((ROWS, COLS),...]
    gather x5 -> x0, local copies, waits for them, and re-layouts: 5.01 us -> none  [the longest x3 3 us: on_device(): from_partner(projected, 'wide', level_bit)[level_perm[level_bit]]]
    slice x5 -> x0, local copies, waits for them, and re-layouts: 2.35 us -> none  [the longest x1 1.56 us: on_device(): position = target + 2 + near_index[target, slot]]
    unnamed x8 -> x12, local copies, waits for them, and re-layouts: 0.03 us -> 2.24 us
    concatenate x1 -> x0, other arithmetic: 1.43 us -> none  [with_halo(): jnp.concatenate([jnp.pad(low, around), x, jnp.pad(high, around)], axis=dim)]
  transfers between devices with their start and end apart: 9 -> 7, of which waited for: 4 -> 5; matrix products, arithmetic and copies ran while one was open for 22% -> 0% of each run, Pallas kernels for 0% -> 7%
where the time goes in v1:
time: 83.2 us; the launch traced here: 82.8 us
  waiting for transfers between devices  42.9 us (52%)
  starting transfers between devices  28.3 us (34%)
  Pallas kernels  8.37 us (10%)
  local copies, waits for them, and re-layouts  2.95 us (4%)
    ppermute x5, waiting for transfers between devices, from_partner(): return lax.ppermute(block, axis, [(i, i ^ 1 << bit) for i in range(count)])  42.9 us
    ppermute x5, starting transfers between devices, from_partner(): return lax.ppermute(block, axis, [(i, i ^ 1 << bit) for i in range(count)])  13.3 us
    ppermute x1, starting transfers between devices, on_device(): high = lax.ppermute(pack, axes, down)  13.1 us
    pallas_call x1, Pallas kernels, near_field(): pl.pallas_call(near_kernel, out_shape=jax.ShapeDtypeStruct((ROWS, COLS),...  4.27 us
    pallas_call x1, Pallas kernels, final_step(): pl.pallas_call(final_kernel, grid=(ROWS // block,), out_shape=jax.ShapeDt...  2.34 us
    unnamed x12, local copies, waits for them, and re-layouts  2.24 us
    ppermute x1, starting transfers between devices, on_device(): low = lax.ppermute(pack, axes, up)  1.92 us
  transfers between devices with their start and end apart: 7, of which 5 were waited for; matrix products, arithmetic and copies ran while one was open for 0% of the time, Pallas kernels for 7%

profile of v1, /device:TPU:1, one launch (start us, length us, event | category | flops | bytes accessed | tf_op | source)
XLA Modules:
  0.0 82.8 jit_solution(542977679956931201)
XLA Ops:
  0.0 0.7 reshape.3.coords_ref
  0.7 1.2 %copy-done = bf16[1024,512]{1,0:T(8,128)(2,1)S(1)} copy-done((bf16[1024,512]{1,0:T(8,128)(2,1)S(1)}, bf16[1024,512]{1,0:T(8,128)(2,1)}, u32[]{:S(2)}) %copy-start) | copy-done | bytes 1048600
  1.9 1.0 %copy-done.2 = bf16[2,512,192]{1,2,0:T(8,128)(2,1)S(1)} copy-done((bf16[2,512,192]{1,2,0:T(8,128)(2,1)S(1)}, bf16[2,512,192]{1,2,0:T(8,128)(2,1)}, u32[]{:S(2)}) %copy-start.2) | copy-done | bytes 393240
  2.9 0.4 project.1
  3.3 13.1 %collective-permute-start.6 = (bf16[1040,512]{1,0:T(8,128)(2,1)S(1)}, bf16[1040,512]{1,0:T(8,128)(2,1)S(1)}, u32[]{:S(2)}, u32[]{:S(2)}) collective-permute-start(bf16[1040,512]{1,0:T(8,128)(2,1)S(1)} %get-tuple-element.12.own_ref), channel_id=1, source_target_pairs={{1,0},{2,1},{3,2},{4,3},{5,4},{6,5},{7,6},{8,7},{9,8},{10,9},{11,1... | collective-permute-start | bytes 3194888 | tf_op jit(solution)/shard_map/ppermute | solution.py:190
  16.4 1.9 %collective-permute-start.5 = (bf16[1040,512]{1,0:T(8,128)(2,1)S(1)}, bf16[1040,512]{1,0:T(8,128)(2,1)S(1)}, u32[]{:S(2)}, u32[]{:S(2)}) collective-permute-start(bf16[1040,512]{1,0:T(8,128)(2,1)S(1)} %get-tuple-element.12.own_ref), channel_id=1, source_target_pairs={{0,1},{1,2},{2,3},{3,4},{4,5},{5,6},{6,7},{7,8},{8,9},{9,10},{10,1... | collective-permute-start | bytes 3194888 | tf_op jit(solution)/shard_map/ppermute | solution.py:189
  18.4 1.9 %collective-permute-start = (bf16[192,512]{1,0:T(8,128)(2,1)S(1)}, bf16[192,512]{1,0:T(8,128)(2,1)S(1)}, u32[]{:S(2)}, u32[]{:S(2)}) collective-permute-start(bf16[192,512]{1,0:T(8,128)(2,1)S(1)} %get-tuple-element.10.own_ref), channel_id=1, source_target_pairs={{0,16},{16,0},{32,48},{48,32},{64,80},{80,64},{96,112},{112,96},{1... | collective-permute-start | bytes 589832 | tf_op jit(solution)/shard_map/ppermute | solution.py:179
  20.3 0.4 prepare.1
  20.7 1.0 %collective-permute-done.other_ref = bf16[192,512]{1,0:T(8,128)(2,1)S(1)} collective-permute-done((bf16[192,512]{1,0:T(8,128)(2,1)S(1)}, bf16[192,512]{1,0:T(8,128)(2,1)S(1)}, u32[]{:S(2)}, u32[]{:S(2)}) %collective-permute-start) | collective-permute-done | bytes 196640 | tf_op jit(solution)/shard_map/ppermute | solution.py:179
  21.7 0.2 level0.1.own_ref
  22.0 4.4 %collective-permute-start.1 = (bf16[192,512]{1,0:T(8,128)(2,1)S(1)}, bf16[192,512]{1,0:T(8,128)(2,1)S(1)}, u32[]{:S(2)}, u32[]{:S(2)}) collective-permute-start(bf16[192,512]{1,0:T(8,128)(2,1)S(1)} %level0.1.own_ref), channel_id=1, source_target_pairs={{0,32},{16,48},{32,0},{48,16},{64,96},{80,112},{96,64},{112,80},{1... | collective-permute-start | bytes 589832 | tf_op jit(solution)/shard_map/ppermute | solution.py:179
  26.3 24.8 %collective-permute-done.1.other_ref = bf16[192,512]{1,0:T(8,128)(2,1)S(1)} collective-permute-done((bf16[192,512]{1,0:T(8,128)(2,1)S(1)}, bf16[192,512]{1,0:T(8,128)(2,1)S(1)}, u32[]{:S(2)}, u32[]{:S(2)}) %collective-permute-start.1) | collective-permute-done | bytes 196640 | tf_op jit(solution)/shard_map/ppermute | solution.py:179
  51.1 0.3 level1.1.own_ref
  51.4 3.2 %collective-permute-start.2 = (bf16[192,512]{1,0:T(8,128)(2,1)S(1)}, bf16[192,512]{1,0:T(8,128)(2,1)S(1)}, u32[]{:S(2)}, u32[]{:S(2)}) collective-permute-start(bf16[192,512]{1,0:T(8,128)(2,1)S(1)} %level1.1.own_ref), channel_id=1, source_target_pairs={{0,64},{16,80},{32,96},{48,112},{64,0},{80,16},{96,32},{112,48},{1... | collective-permute-start | bytes 589832 | tf_op jit(solution)/shard_map/ppermute | solution.py:179
  54.6 4.7 %collective-permute-done.2.other_ref = bf16[192,512]{1,0:T(8,128)(2,1)S(1)} collective-permute-done((bf16[192,512]{1,0:T(8,128)(2,1)S(1)}, bf16[192,512]{1,0:T(8,128)(2,1)S(1)}, u32[]{:S(2)}, u32[]{:S(2)}) %collective-permute-start.2) | collective-permute-done | bytes 196640 | tf_op jit(solution)/shard_map/ppermute | solution.py:179
  59.3 0.2 level2.1.own_ref
  59.5 0.0 copy-start.5
  59.5 1.9 %collective-permute-start.3 = (bf16[192,512]{1,0:T(8,128)(2,1)S(1)}, bf16[192,512]{1,0:T(8,128)(2,1)S(1)}, u32[]{:S(2)}, u32[]{:S(2)}) collective-permute-start(bf16[192,512]{1,0:T(8,128)(2,1)S(1)} %level2.1.own_ref), channel_id=1, source_target_pairs={{0,1},{1,0},{2,3},{3,2},{4,5},{5,4},{6,7},{7,6},{8,9},{9,8},{10,11... | collective-permute-start | bytes 589832 | tf_op jit(solution)/shard_map/ppermute | solution.py:179
  61.5 5.1 %collective-permute-done.3.other_ref = bf16[192,512]{1,0:T(8,128)(2,1)S(1)} collective-permute-done((bf16[192,512]{1,0:T(8,128)(2,1)S(1)}, bf16[192,512]{1,0:T(8,128)(2,1)S(1)}, u32[]{:S(2)}, u32[]{:S(2)}) %collective-permute-start.3) | collective-permute-done | bytes 196640 | tf_op jit(solution)/shard_map/ppermute | solution.py:179
  66.5 0.2 level3.1.own_ref
  66.8 1.9 %collective-permute-start.4 = (bf16[192,512]{1,0:T(8,128)(2,1)S(1)}, bf16[192,512]{1,0:T(8,128)(2,1)S(1)}, u32[]{:S(2)}, u32[]{:S(2)}) collective-permute-start(bf16[192,512]{1,0:T(8,128)(2,1)S(1)} %level3.1.own_ref), channel_id=1, source_target_pairs={{0,2},{1,3},{2,0},{3,1},{4,6},{5,7},{6,4},{7,5},{8,10},{9,11},{10,... | collective-permute-start | bytes 589832 | tf_op jit(solution)/shard_map/ppermute | solution.py:179
  68.8 4.3 %near.1.near_ref = f32[1024,512]{1,0:T(8,128)S(1)} custom-call(s32[2,3]{1,0:T(2,128)S(1)} %copy-done.5, bf16[1040,512]{1,0:T(8,128)(2,1)S(1)} %get-tuple-element.12.own_ref, bf16[1040,512]{1,0:T(8,128)(2,1)S(1)} %collective-permute-done.5.low_ref, bf16[1040,512]{1,0:T(8,128)(2,1)S(1)} %collective-permute-done.6.high_ref), custom_call_target="tpu_custom_call" | custom-call | tf_op jit(solution)/shard_map/near/pallas_call | solution.py:136
  73.0 7.4 %collective-permute-done.4.other_ref = bf16[192,512]{1,0:T(8,128)(2,1)S(1)} collective-permute-done((bf16[192,512]{1,0:T(8,128)(2,1)S(1)}, bf16[192,512]{1,0:T(8,128)(2,1)S(1)}, u32[]{:S(2)}, u32[]{:S(2)}) %collective-permute-start.4) | collective-permute-done | bytes 196640 | tf_op jit(solution)/shard_map/ppermute | solution.py:179
  80.4 2.3 %final.1 = bf16[1024,512]{1,0:T(8,128)(2,1)} custom-call(bf16[5,2,192,192]{3,2,1,0:T(8,128)(2,1)S(1)} %get-tuple-element.9.t_ref, bf16[192,512]{1,0:T(8,128)(2,1)S(1)} %level3.1.own_ref, bf16[192,512]{1,0:T(8,128)(2,1)S(1)} %collective-permute-done.4.other_ref, bf16[1024,192]{1,0:T(8,128)(2,1)S(1)} %get-tuple-element.11.e_ref, f32[1024,512]{1,0:T(8,128)S(1)} %near.1.near_ref), custom_call_target="tpu_custom_call" | custom-call | tf_op jit(solution)/shard_map/final/pallas_call | solution.py:159
  (11 shorter events, 0.0 us)
Async XLA Ops:
  0.0 20.3 %copy-start.4 = (s32[5,192]{1,0:T(8,128)S(1)}, s32[5,192]{1,0:T(8,128)}, u32[]{:S(2)}) copy-start(s32[5,192]{1,0:T(8,128)} %perm_ref.1) | copy-start | bytes 11524
  0.7 1.2 %copy-start = (bf16[1024,512]{1,0:T(8,128)(2,1)S(1)}, bf16[1024,512]{1,0:T(8,128)(2,1)}, u32[]{:S(2)}) copy-start(bf16[1024,512]{1,0:T(8,128)(2,1)} %x_ref.1) | copy-start | bytes 3145732
  1.9 1.0 %copy-start.2 = (bf16[2,512,192]{1,2,0:T(8,128)(2,1)S(1)}, bf16[2,512,192]{1,2,0:T(8,128)(2,1)}, u32[]{:S(2)}) copy-start(bf16[2,512,192]{1,2,0:T(8,128)(2,1)} %param.10) | copy-start | bytes 1179652
  2.9 17.4 %copy-start.1 = (bf16[1,5,2,192,192]{4,3,2,1,0:T(8,128)(2,1)S(1)}, bf16[1,5,2,192,192]{4,3,2,1,0:T(8,128)(2,1)}, u32[]{:S(2)}) copy-start(bf16[1,5,2,192,192]{4,3,2,1,0:T(8,128)(2,1)} %param.12) | copy-start | bytes 2211844
  2.9 17.4 %copy-start.3 = (bf16[2,512,192]{1,2,0:T(8,128)(2,1)S(1)}, bf16[2,512,192]{1,2,0:T(8,128)(2,1)}, u32[]{:S(2)}) copy-start(bf16[2,512,192]{1,2,0:T(8,128)(2,1)} %param.11) | copy-start | bytes 1179652
  3.3 65.4 %collective-permute-start.6 = (bf16[1040,512]{1,0:T(8,128)(2,1)S(1)}, bf16[1040,512]{1,0:T(8,128)(2,1)S(1)}, u32[]{:S(2)}, u32[]{:S(2)}) collective-permute-start(bf16[1040,512]{1,0:T(8,128)(2,1)S(1)} %get-tuple-element.12.own_ref), channel_id=1, source_target_pairs={{1,0},{2,1},{3,2},{4,3},{5,4},{6,5},{7,6},{8,7},{9,8},{10,9},{11,1... | collective-permute-start | bytes 3194888 | tf_op jit(solution)/shard_map/ppermute | solution.py:190
  16.4 52.3 %collective-permute-start.5 = (bf16[1040,512]{1,0:T(8,128)(2,1)S(1)}, bf16[1040,512]{1,0:T(8,128)(2,1)S(1)}, u32[]{:S(2)}, u32[]{:S(2)}) collective-permute-start(bf16[1040,512]{1,0:T(8,128)(2,1)S(1)} %get-tuple-element.12.own_ref), channel_id=1, source_target_pairs={{0,1},{1,2},{2,3},{3,4},{4,5},{5,6},{6,7},{7,8},{8,9},{9,10},{10,1... | collective-permute-start | bytes 3194888 | tf_op jit(solution)/shard_map/ppermute | solution.py:189
  18.4 3.3 %collective-permute-start = (bf16[192,512]{1,0:T(8,128)(2,1)S(1)}, bf16[192,512]{1,0:T(8,128)(2,1)S(1)}, u32[]{:S(2)}, u32[]{:S(2)}) collective-permute-start(bf16[192,512]{1,0:T(8,128)(2,1)S(1)} %get-tuple-element.10.own_ref), channel_id=1, source_target_pairs={{0,16},{16,0},{32,48},{48,32},{64,80},{80,64},{96,112},{112,96},{1... | collective-permute-start | bytes 589832 | tf_op jit(solution)/shard_map/ppermute | solution.py:179
  22.0 29.1 %collective-permute-start.1 = (bf16[192,512]{1,0:T(8,128)(2,1)S(1)}, bf16[192,512]{1,0:T(8,128)(2,1)S(1)}, u32[]{:S(2)}, u32[]{:S(2)}) collective-permute-start(bf16[192,512]{1,0:T(8,128)(2,1)S(1)} %level0.1.own_ref), channel_id=1, source_target_pairs={{0,32},{16,48},{32,0},{48,16},{64,96},{80,112},{96,64},{112,80},{1... | collective-permute-start | bytes 589832 | tf_op jit(solution)/shard_map/ppermute | solution.py:179
  51.4 7.9 %collective-permute-start.2 = (bf16[192,512]{1,0:T(8,128)(2,1)S(1)}, bf16[192,512]{1,0:T(8,128)(2,1)S(1)}, u32[]{:S(2)}, u32[]{:S(2)}) collective-permute-start(bf16[192,512]{1,0:T(8,128)(2,1)S(1)} %level1.1.own_ref), channel_id=1, source_target_pairs={{0,64},{16,80},{32,96},{48,112},{64,0},{80,16},{96,32},{112,48},{1... | collective-permute-start | bytes 589832 | tf_op jit(solution)/shard_map/ppermute | solution.py:179
  59.5 9.2 %copy-start.5 = (s32[2,3]{1,0:T(2,128)S(1)}, s32[2,3]{1,0:T(2,128)}, u32[]{:S(2)}) copy-start(s32[2,3]{1,0:T(2,128)} %index_ref.1) | copy-start | bytes 76
  59.5 7.0 %collective-permute-start.3 = (bf16[192,512]{1,0:T(8,128)(2,1)S(1)}, bf16[192,512]{1,0:T(8,128)(2,1)S(1)}, u32[]{:S(2)}, u32[]{:S(2)}) collective-permute-start(bf16[192,512]{1,0:T(8,128)(2,1)S(1)} %level2.1.own_ref), channel_id=1, source_target_pairs={{0,1},{1,0},{2,3},{3,2},{4,5},{5,4},{6,7},{7,6},{8,9},{9,8},{10,11... | collective-permute-start | bytes 589832 | tf_op jit(solution)/shard_map/ppermute | solution.py:179
  66.8 13.6 %collective-permute-start.4 = (bf16[192,512]{1,0:T(8,128)(2,1)S(1)}, bf16[192,512]{1,0:T(8,128)(2,1)S(1)}, u32[]{:S(2)}, u32[]{:S(2)}) collective-permute-start(bf16[192,512]{1,0:T(8,128)(2,1)S(1)} %level3.1.own_ref), channel_id=1, source_target_pairs={{0,2},{1,3},{2,0},{3,1},{4,6},{5,7},{6,4},{7,5},{8,10},{9,11},{10,... | collective-permute-start | bytes 589832 | tf_op jit(solution)/shard_map/ppermute | solution.py:179

commit v2 on v1

--- a/solution.py
+++ b/solution.py
@@ -15,66 +15,125 @@
 COLS = 512
 ROWS = 1024
 PACK = ROWS + 16
+COVER = 30_000_000_000
 SOFT = 0.0004
 FACTOR = 0.25 / math.sqrt(LEAF)
 F32 = jnp.float32
 BF16 = jnp.bfloat16
 VMEM = pl.BlockSpec(memory_space=pltpu.VMEM)
+HBM = pl.BlockSpec(memory_space=pltpu.HBM)
 SMEM = pl.BlockSpec(memory_space=pltpu.SMEM)
+
+
+def in_hbm(array):
+    return pltpu.with_memory_space_constraint(array, pltpu.HBM)
 
 
 def params():
     return pltpu.CompilerParams(vmem_limit_bytes=40 << 20)
 
 
-def project_kernel(x_ref, basis_ref, coords_ref, s_ref, pack_ref):
-    total = jnp.dot(basis_ref[0], x_ref[:LEAF, :], preferred_element_type=F32)
-    total = total + jnp.dot(basis_ref[1], x_ref[LEAF:, :], preferred_element_type=F32)
+def folded(matrix, perm_row):
+    k = lax.broadcasted_iota(jnp.int32, (RANK, RANK), 0)
+    picked = jnp.where(k == perm_row, 1.0, 0.0).astype(BF16)
+    return lax.dot_general(
+        matrix, picked, (((1,), (1,)), ((), ())), preferred_element_type=F32
+    ).astype(BF16)
+
+
+def project_kernel(
+    x_ref,
+    basis_ref,
+    points_ref,
+    transfer_ref,
+    order_ref,
+    s_ref,
+    pack_ref,
+    t_ref,
+    b_ref,
+    coords_ref,
+    perm_ref,
+    sems,
+):
+    copies = []
+    for leaf in range(2):
+        block = pl.ds(leaf * LEAF, LEAF)
+        copies.append(
+            (
+                pltpu.make_async_copy(basis_ref.at[leaf], b_ref.at[leaf], sems.at[2 * leaf]),
+                pltpu.make_async_copy(
+                    x_ref.at[block], pack_ref.at[block], sems.at[2 * leaf + 1]
+                ),
+            )
+        )
+    points = pltpu.make_async_copy(points_ref, coords_ref, sems.at[4])
+    first = pltpu.make_async_copy(transfer_ref.at[0], t_ref.at[0], sems.at[5])
+    order = pltpu.make_async_copy(order_ref, perm_ref, sems.at[6])
+    for pair in copies:
+        for copy in pair:
+            copy.start()
+    points.start()
+    first.start()
+    order.start()
+    points.wait()
+    pack_ref[ROWS:, :] = jnp.concatenate(
+        [coords_ref[0], coords_ref[1], jnp.zeros((12, COLS), BF16)], axis=0
+    )
+    total = None
+    for leaf in range(2):
+        for copy in copies[leaf]:
+            copy.wait()
+        part = jnp.dot(
+            b_ref[leaf], pack_ref[leaf * LEAF : (leaf + 1) * LEAF, :], preferred_element_type=F32
+        )
+        total = part if total is None else total + part
     s_ref[...] = total.astype(BF16)
-    pack_ref[:ROWS, :] = x_ref[...]
-    pack_ref[ROWS:, :] = jnp.concatenate(
-        [coords_ref[...], jnp.zeros((12, COLS), BF16)], axis=0
-    )
-
-
-def project(x, basis_t, coords4):
+    first.wait()
+    order.wait()
+    t_ref[0, 1] = folded(t_ref[0, 1], perm_ref[0:1, :])
+
+
+def project(x, basis_t, coords, transfer, perm):
     return pl.pallas_call(
         project_kernel,
         out_shape=(
             jax.ShapeDtypeStruct((RANK, COLS), BF16),
             jax.ShapeDtypeStruct((PACK, COLS), BF16),
+            jax.ShapeDtypeStruct((1, 2, RANK, RANK), BF16),
         ),
-        in_specs=[VMEM, VMEM, VMEM],
-        out_specs=(VMEM, VMEM),
+        in_specs=[HBM] * 5,
+        out_specs=(VMEM, VMEM, VMEM),
+        scratch_shapes=[
+            pltpu.VMEM((2, RANK, LEAF), BF16),
+            pltpu.VMEM((2, 2, LEAF), BF16),
+            pltpu.VMEM((LEVELS, RANK), jnp.int32),
+            pltpu.SemaphoreType.DMA((7,)),
+        ],
         compiler_params=params(),
         name="project",
-    )(x, basis_t, coords4)
-
-
-def prepare_kernel(transfer_ref, perm_ref, expand_ref, t_ref, e_ref):
-    k = lax.broadcasted_iota(jnp.int32, (RANK, RANK), 0)
-    for level in range(LEVELS):
-        t_ref[level, 0] = transfer_ref[level, 0]
-        picked = jnp.where(k == perm_ref[level : level + 1, :], 1.0, 0.0).astype(BF16)
-        t_ref[level, 1] = lax.dot_general(
-            transfer_ref[level, 1], picked, (((1,), (1,)), ((), ())), preferred_element_type=F32
-        ).astype(BF16)
+    )(*(in_hbm(array) for array in (x, basis_t, coords, transfer, perm)))
+
+
+def prepare_kernel(transfer_ref, perm_ref, expand_ref, after_ref, t_ref, e_ref):
+    for level in range(1, LEVELS):
+        t_ref[level - 1, 0] = transfer_ref[level, 0]
+        t_ref[level - 1, 1] = folded(transfer_ref[level, 1], perm_ref[level : level + 1, :])
     for leaf in range(2):
         e_ref[leaf * LEAF : (leaf + 1) * LEAF, :] = expand_ref[leaf].T
 
 
-def prepare(transfer, perm, expand_t):
+def prepare(transfer, perm, expand_t, after):
     return pl.pallas_call(
         prepare_kernel,
         out_shape=(
-            jax.ShapeDtypeStruct((LEVELS, 2, RANK, RANK), BF16),
+            jax.ShapeDtypeStruct((LEVELS - 1, 2, RANK, RANK), BF16),
             jax.ShapeDtypeStruct((ROWS, RANK), BF16),
         ),
-        in_specs=[VMEM, VMEM, VMEM],
+        in_specs=[VMEM, VMEM, VMEM, VMEM],
         out_specs=(VMEM, VMEM),
         compiler_params=params(),
         name="prepare",
-    )(transfer, perm, expand_t)
+    )(transfer, perm, expand_t, after)
 
 
 def level_kernel(t_ref, own_ref, other_ref, s_ref):
@@ -83,20 +142,34 @@
     s_ref[...] = total.astype(BF16)
 
 
-def level_step(level, t, own, other):
-    return pl.pallas_call(
-        level_kernel,
+def gathered_kernel(high_ref, t_ref, own_ref, both_ref, s_ref):
+    total = jnp.dot(t_ref[0, 0], own_ref[...], preferred_element_type=F32)
+    total = total + jnp.dot(
+        t_ref[0, 1], both_ref[1 - high_ref[0]], preferred_element_type=F32
+    )
+    s_ref[...] = total.astype(BF16)
+
+
+def level_step(t, index, own, other, high=None, weight=4 * RANK * RANK * COLS):
+    flat = pl.BlockSpec((RANK, COLS), lambda i: (0, 0))
+    specs = [pl.BlockSpec((1, 2, RANK, RANK), lambda i: (index, 0, 0, 0)), flat]
+    if high is None:
+        body, specs, args = level_kernel, specs + [flat], (t, own, other)
+    else:
+        both = pl.BlockSpec((2, RANK, COLS), lambda i: (0, 0, 0))
+        body, specs, args = gathered_kernel, [SMEM] + specs + [both], (high, t, own, other)
+    return pl.pallas_call(
+        body,
         grid=(1,),
         out_shape=jax.ShapeDtypeStruct((RANK, COLS), BF16),
-        in_specs=[
-            pl.BlockSpec((1, 2, RANK, RANK), lambda i: (level, 0, 0, 0)),
-            pl.BlockSpec((RANK, COLS), lambda i: (0, 0)),
-            pl.BlockSpec((RANK, COLS), lambda i: (0, 0)),
-        ],
-        out_specs=pl.BlockSpec((RANK, COLS), lambda i: (0, 0)),
-        compiler_params=params(),
-        name=f"level{level}",
-    )(t, own, other)
+        in_specs=specs,
+        out_specs=flat,
+        compiler_params=params(),
+        cost_estimate=pl.CostEstimate(
+            flops=weight, transcendentals=0, bytes_accessed=6 * RANK * COLS
+        ),
+        name=f"level_{index}",
+    )(*args)
 
 
 def near_kernel(index_ref, own_ref, low_ref, high_ref, near_ref):
@@ -161,7 +234,7 @@
         grid=(ROWS // block,),
         out_shape=jax.ShapeDtypeStruct((ROWS, COLS), BF16),
         in_specs=[
-            pl.BlockSpec((1, 2, RANK, RANK), lambda i: (LEVELS - 1, 0, 0, 0)),
+            pl.BlockSpec((1, 2, RANK, RANK), lambda i: (LEVELS - 2, 0, 0, 0)),
             pl.BlockSpec((RANK, COLS), lambda i: (0, 0)),
             pl.BlockSpec((RANK, COLS), lambda i: (0, 0)),
             pl.BlockSpec((block, RANK), lambda i: (i, 0)),
@@ -179,22 +252,34 @@
     return lax.ppermute(block, axis, [(i, i ^ (1 << bit)) for i in range(count)])
 
 
+def with_partner(block, axis, bit):
+    count = lax.axis_size(axis)
+    pairs = [[i, i | 1 << bit] for i in range(count) if not i >> bit & 1]
+    both = lax.all_gather(block, axis, axis_index_groups=pairs)
+    high = (lax.axis_index(axis) >> bit & 1).reshape(1)
+    return both, high
+
+
 def on_device(rhs, coords, near_index, project_basis, expand_basis, transfer, level_perm):
     axes = ("wide", "pair")
     devices = lax.axis_size("wide") * lax.axis_size("pair")
     up = [(i, i + 1) for i in range(devices - 1)]
     down = [(i + 1, i) for i in range(devices - 1)]
-    s, pack = project(rhs, jnp.swapaxes(project_basis, 1, 2), coords.reshape(4, LEAF))
-    partner = from_partner(s, "wide", 0)
-    low = lax.ppermute(pack, axes, up)
-    high = lax.ppermute(pack, axes, down)
-    t, e = prepare(transfer[0], level_perm, jnp.swapaxes(expand_basis, 1, 2))
-    for level in range(LEVELS - 1):
-        s = level_step(level, t, s, partner)
-        if level + 1 < LW:
-            partner = from_partner(s, "wide", level + 1)
-        else:
-            partner = from_partner(s, "pair", level + 1 - LW)
+    s, pack, t0 = project(
+        rhs, jnp.swapaxes(project_basis, 1, 2), coords, transfer[0], level_perm
+    )
+    both, high_bit = with_partner(s, "wide", 0)
+    s = level_step(t0, 0, s, both, high_bit)
+    partner = from_partner(s, "wide", 1)
+    t, e = prepare(transfer[0], level_perm, jnp.swapaxes(expand_basis, 1, 2), s)
+    sent, e = lax.optimization_barrier((pack, e))
+    low = lax.ppermute(sent, axes, up)
+    high = lax.ppermute(sent, axes, down)
+    s = level_step(t, 0, s, partner, weight=COVER)
+    s = level_step(t, 1, s, from_partner(s, "wide", 2))
+    both, high_bit = with_partner(s, "pair", 0)
+    s = level_step(t, 2, s, both, high_bit)
+    partner = from_partner(s, "pair", 1)
     near = near_field(near_index, pack, low, high)
     return final_step(t, s, partner, e, near)
 

time: 83.2 us -> 67.8 us (0.81)
  the two profiles are of different devices: /device:TPU:1 before, /device:TPU:16 now
where the time goes in v2:
time: 67.8 us; the launch traced here: 67.4 us
  starting transfers between devices  23.1 us (34%)
  waiting for transfers between devices  19.4 us (29%)
  blocking collectives  12.8 us (19%)
  Pallas kernels  11 us (16%)
  local copies, waits for them, and re-layouts  1.01 us (1%)
    ppermute x3, waiting for transfers between devices, from_partner(): return lax.ppermute(block, axis, [(i, i ^ 1 << bit) for i in range(count)])  19.4 us
    all_gather x2, blocking collectives, with_partner(): both = lax.all_gather(block, axis, axis_index_groups=pairs)  12.8 us
    ppermute x1, starting transfers between devices, on_device(): high = lax.ppermute(sent, axes, down)  10.9 us
    ppermute x3, starting transfers between devices, from_partner(): return lax.ppermute(block, axis, [(i, i ^ 1 << bit) for i in range(count)])  10.3 us
    pallas_call x1, Pallas kernels, near_field(): pl.pallas_call(near_kernel, out_shape=jax.ShapeDtypeStruct((ROWS, COLS),...  5.26 us
    pallas_call x1, Pallas kernels, final_step(): pl.pallas_call(final_kernel, grid=(ROWS // block,), out_shape=jax.ShapeDt...  2.34 us
    pallas_call x1, Pallas kernels, project(): pl.pallas_call(project_kernel, out_shape=(jax.ShapeDtypeStruct((RANK, COL...  2 us
    ppermute x1, starting transfers between devices, on_device(): low = lax.ppermute(sent, axes, up)  1.92 us
  transfers between devices with their start and end apart: 5, of which 2 were waited for; matrix products, arithmetic and copies ran while one was open for 0% of the time, Pallas kernels for 9%

profile of v2, /device:TPU:16, one launch (start us, length us, event | category | flops | bytes accessed | tf_op | source)
XLA Modules:
  0.0 67.4 jit_solution(9142473899786897778)
XLA Ops:
  0.0 2.0 %project.1 = (bf16[192,512]{1,0:T(8,128)(2,1)S(1)}, bf16[1040,512]{1,0:T(8,128)(2,1)S(1)}, bf16[1,2,192,192]{3,2,1,0:T(8,128)(2,1)S(1)}) custom-call(bf16[1024,512]{1,0:T(8,128)(2,1)} %x_ref.1, bf16[2,192,512]{2,1,0:T(8,128)(2,1)} %bitcast.12, bf16[2,2,512]{2,1,0:T(2,128)(2,1)} %points_ref.1, bf16[5,2,192,192]{3,2,1,0:T(8,128)(2,1)} %bitcast.7, ...), custom_call_target="tpu_custom_call" | custom-call | tf_op jit(solution)/shard_map/project/pallas_call | solution.py:97
  2.0 0.0 copy-start
  2.0 0.0 copy-start.2
  2.0 2.2 %all-gather = bf16[384,512]{1,0:T(8,128)(2,1)S(1)} all-gather(bf16[192,512]{1,0:T(8,128)(2,1)S(1)} %get-tuple-element.13.own_ref), channel_id=2, replica_groups={{0,16},{32,48},{64,80},{96,112},{128,144},{160,176},{192,208},{224,240}..., dimensions={0}, use_global_device_ids=true | all-gather | bytes 589824 | tf_op jit(solution)/shard_map/all_gather | solution.py:258
  4.3 0.2 level_0.2.after_ref.own_ref
  4.5 4.9 %collective-permute-start = (bf16[192,512]{1,0:T(8,128)(2,1)S(1)}, bf16[192,512]{1,0:T(8,128)(2,1)S(1)}, u32[]{:S(2)}, u32[]{:S(2)}) collective-permute-start(bf16[192,512]{1,0:T(8,128)(2,1)S(1)} %level_0.2.after_ref.own_ref), channel_id=1, source_target_pairs={{0,32},{16,48},{32,0},{48,16},{64,96},{80,112},{96,64},{112,80},{1... | collective-permute-start | bytes 589832 | tf_op jit(solution)/shard_map/ppermute | solution.py:252
  9.5 0.0 copy-start.1
  9.5 1.0 %copy-done.1 = bf16[2,512,192]{1,2,0:T(8,128)(2,1)S(1)} copy-done((bf16[2,512,192]{1,2,0:T(8,128)(2,1)S(1)}, bf16[2,512,192]{1,2,0:T(8,128)(2,1)}, u32[]{:S(2)}) %copy-start.1) | copy-done | bytes 393240
  10.5 0.4 prepare.1
  10.8 10.9 %collective-permute-start.4 = (bf16[1040,512]{1,0:T(8,128)(2,1)S(1)}, bf16[1040,512]{1,0:T(8,128)(2,1)}, u32[]{:S(2)}, u32[]{:S(2)}) collective-permute-start(bf16[1040,512]{1,0:T(8,128)(2,1)S(1)} %get-tuple-element.18.own_ref), channel_id=1, source_target_pairs={{1,0},{2,1},{3,2},{4,3},{5,4},{6,5},{7,6},{8,7},{9,8},{10,9},{11,1... | collective-permute-start | bytes 3194888 | tf_op jit(solution)/shard_map/ppermute | solution.py:277
  21.7 1.9 %collective-permute-start.3 = (bf16[1040,512]{1,0:T(8,128)(2,1)S(1)}, bf16[1040,512]{1,0:T(8,128)(2,1)}, u32[]{:S(2)}, u32[]{:S(2)}) collective-permute-start(bf16[1040,512]{1,0:T(8,128)(2,1)S(1)} %get-tuple-element.18.own_ref), channel_id=1, source_target_pairs={{0,1},{1,2},{2,3},{3,4},{4,5},{5,6},{6,7},{7,8},{8,9},{9,10},{10,1... | collective-permute-start | bytes 3194888 | tf_op jit(solution)/shard_map/ppermute | solution.py:276
  23.7 0.0 collective-permute-done.other_ref
  23.7 0.2 level_0.3.own_ref
  23.9 3.5 %collective-permute-start.1 = (bf16[192,512]{1,0:T(8,128)(2,1)S(1)}, bf16[192,512]{1,0:T(8,128)(2,1)S(1)}, u32[]{:S(2)}, u32[]{:S(2)}) collective-permute-start(bf16[192,512]{1,0:T(8,128)(2,1)S(1)} %level_0.3.own_ref), channel_id=1, source_target_pairs={{0,64},{16,80},{32,96},{48,112},{64,0},{80,16},{96,32},{112,48},{1... | collective-permute-start | bytes 589832 | tf_op jit(solution)/shard_map/ppermute | solution.py:252
  27.4 13.1 %collective-permute-done.1.other_ref = bf16[192,512]{1,0:T(8,128)(2,1)S(1)} collective-permute-done((bf16[192,512]{1,0:T(8,128)(2,1)S(1)}, bf16[192,512]{1,0:T(8,128)(2,1)S(1)}, u32[]{:S(2)}, u32[]{:S(2)}) %collective-permute-start.1) | collective-permute-done | bytes 196640 | tf_op jit(solution)/shard_map/ppermute | solution.py:252
  40.5 0.3 level_1.1.own_ref
  40.7 0.0 copy-start.3
  40.8 10.5 %all-gather.1 = bf16[384,512]{1,0:T(8,128)(2,1)S(1)} all-gather(bf16[192,512]{1,0:T(8,128)(2,1)S(1)} %level_1.1.own_ref), channel_id=3, replica_groups={{0,1},{2,3},{4,5},{6,7},{8,9},{10,11},{12,13},{14,15},{16,17},{18,19},{..., dimensions={0}, use_global_device_ids=true | all-gather | bytes 589824 | tf_op jit(solution)/shard_map/all_gather | solution.py:258
  51.3 0.3 level_2.1.own_ref
  51.6 1.9 %collective-permute-start.2 = (bf16[192,512]{1,0:T(8,128)(2,1)S(1)}, bf16[192,512]{1,0:T(8,128)(2,1)S(1)}, u32[]{:S(2)}, u32[]{:S(2)}) collective-permute-start(bf16[192,512]{1,0:T(8,128)(2,1)S(1)} %level_2.1.own_ref), channel_id=1, source_target_pairs={{0,2},{1,3},{2,0},{3,1},{4,6},{5,7},{6,4},{7,5},{8,10},{9,11},{10,... | collective-permute-start | bytes 589832 | tf_op jit(solution)/shard_map/ppermute | solution.py:252
  53.5 0.0 collective-permute-done.4.high_ref
  53.5 5.3 %near.1.near_ref = f32[1024,512]{1,0:T(8,128)S(1)} custom-call(s32[2,3]{1,0:T(2,128)S(1)} %copy-done.3, bf16[1040,512]{1,0:T(8,128)(2,1)S(1)} %get-tuple-element.18.own_ref, bf16[1040,512]{1,0:T(8,128)(2,1)} %collective-permute-done.3.low_ref, bf16[1040,512]{1,0:T(8,128)(2,1)} %collective-permute-done.4.high_ref), custom_call_target="tpu_custom_call" | custom-call | tf_op jit(solution)/shard_map/near/pallas_call | solution.py:209
  58.8 6.3 %collective-permute-done.2.other_ref = bf16[192,512]{1,0:T(8,128)(2,1)S(1)} collective-permute-done((bf16[192,512]{1,0:T(8,128)(2,1)S(1)}, bf16[192,512]{1,0:T(8,128)(2,1)S(1)}, u32[]{:S(2)}, u32[]{:S(2)}) %collective-permute-start.2) | collective-permute-done | bytes 196640 | tf_op jit(solution)/shard_map/ppermute | solution.py:252
  65.1 2.3 %final.1 = bf16[1024,512]{1,0:T(8,128)(2,1)} custom-call(bf16[4,2,192,192]{3,2,1,0:T(8,128)(2,1)S(1)} %get-tuple-element.14.t_ref, bf16[192,512]{1,0:T(8,128)(2,1)S(1)} %level_2.1.own_ref, bf16[192,512]{1,0:T(8,128)(2,1)S(1)} %collective-permute-done.2.other_ref, bf16[1024,192]{1,0:T(8,128)(2,1)S(1)} %get-tuple-element.17.e_ref, f32[1024,512]{1,0:T(8,128)S(1)} %near.1.near_ref), custom_call_target="tpu_custom_call" | custom-call | tf_op jit(solution)/shard_map/final/pallas_call | solution.py:232
  (4 shorter events, 0.0 us)
Async XLA Ops:
  2.0 7.4 %copy-start = (bf16[1,5,2,192,192]{4,3,2,1,0:T(8,128)(2,1)S(1)}, bf16[1,5,2,192,192]{4,3,2,1,0:T(8,128)(2,1)}, u32[]{:S(2)}) copy-start(bf16[1,5,2,192,192]{4,3,2,1,0:T(8,128)(2,1)} %param.12) | copy-start | bytes 2211844
  2.0 7.4 %copy-start.2 = (s32[5,192]{1,0:T(8,128)S(1)}, s32[5,192]{1,0:T(8,128)}, u32[]{:S(2)}) copy-start(s32[5,192]{1,0:T(8,128)} %perm_ref.1) | copy-start | bytes 11524
  4.5 19.1 %collective-permute-start = (bf16[192,512]{1,0:T(8,128)(2,1)S(1)}, bf16[192,512]{1,0:T(8,128)(2,1)S(1)}, u32[]{:S(2)}, u32[]{:S(2)}) collective-permute-start(bf16[192,512]{1,0:T(8,128)(2,1)S(1)} %level_0.2.after_ref.own_ref), channel_id=1, source_target_pairs={{0,32},{16,48},{32,0},{48,16},{64,96},{80,112},{96,64},{112,80},{1... | collective-permute-start | bytes 589832 | tf_op jit(solution)/shard_map/ppermute | solution.py:252
  9.5 1.0 %copy-start.1 = (bf16[2,512,192]{1,2,0:T(8,128)(2,1)S(1)}, bf16[2,512,192]{1,2,0:T(8,128)(2,1)}, u32[]{:S(2)}) copy-start(bf16[2,512,192]{1,2,0:T(8,128)(2,1)} %param.11) | copy-start | bytes 1179652
  10.8 42.6 %collective-permute-start.4 = (bf16[1040,512]{1,0:T(8,128)(2,1)S(1)}, bf16[1040,512]{1,0:T(8,128)(2,1)}, u32[]{:S(2)}, u32[]{:S(2)}) collective-permute-start(bf16[1040,512]{1,0:T(8,128)(2,1)S(1)} %get-tuple-element.18.own_ref), channel_id=1, source_target_pairs={{1,0},{2,1},{3,2},{4,3},{5,4},{6,5},{7,6},{8,7},{9,8},{10,9},{11,1... | collective-permute-start | bytes 3194888 | tf_op jit(solution)/shard_map/ppermute | solution.py:277
  21.7 31.8 %collective-permute-start.3 = (bf16[1040,512]{1,0:T(8,128)(2,1)S(1)}, bf16[1040,512]{1,0:T(8,128)(2,1)}, u32[]{:S(2)}, u32[]{:S(2)}) collective-permute-start(bf16[1040,512]{1,0:T(8,128)(2,1)S(1)} %get-tuple-element.18.own_ref), channel_id=1, source_target_pairs={{0,1},{1,2},{2,3},{3,4},{4,5},{5,6},{6,7},{7,8},{8,9},{9,10},{10,1... | collective-permute-start | bytes 3194888 | tf_op jit(solution)/shard_map/ppermute | solution.py:276
  23.9 16.6 %collective-permute-start.1 = (bf16[192,512]{1,0:T(8,128)(2,1)S(1)}, bf16[192,512]{1,0:T(8,128)(2,1)S(1)}, u32[]{:S(2)}, u32[]{:S(2)}) collective-permute-start(bf16[192,512]{1,0:T(8,128)(2,1)S(1)} %level_0.3.own_ref), channel_id=1, source_target_pairs={{0,64},{16,80},{32,96},{48,112},{64,0},{80,16},{96,32},{112,48},{1... | collective-permute-start | bytes 589832 | tf_op jit(solution)/shard_map/ppermute | solution.py:252
  40.7 12.8 %copy-start.3 = (s32[2,3]{1,0:T(2,128)S(1)}, s32[2,3]{1,0:T(2,128)}, u32[]{:S(2)}) copy-start(s32[2,3]{1,0:T(2,128)} %index_ref.1) | copy-start | bytes 76
  51.6 13.5 %collective-permute-start.2 = (bf16[192,512]{1,0:T(8,128)(2,1)S(1)}, bf16[192,512]{1,0:T(8,128)(2,1)S(1)}, u32[]{:S(2)}, u32[]{:S(2)}) collective-permute-start(bf16[192,512]{1,0:T(8,128)(2,1)S(1)} %level_2.1.own_ref), channel_id=1, source_target_pairs={{0,2},{1,3},{2,0},{3,1},{4,6},{5,7},{6,4},{7,5},{8,10},{9,11},{10,... | collective-permute-start | bytes 589832 | tf_op jit(solution)/shard_map/ppermute | solution.py:252

commit v3 on v2

--- a/solution.py
+++ b/solution.py
@@ -1,3 +1,4 @@
+import functools
 import math
 
 import jax
@@ -15,13 +16,18 @@
 COLS = 512
 ROWS = 1024
 PACK = ROWS + 16
-COVER = 30_000_000_000
+RUN = 8
+COVER_1 = 3_000_000_000
+COVER_INNER = 5_000_000_000
+COVER_OUTER = 6_000_000_000
+COVER_FAR = 4_000_000_000
 SOFT = 0.0004
 FACTOR = 0.25 / math.sqrt(LEAF)
 F32 = jnp.float32
 BF16 = jnp.bfloat16
 VMEM = pl.BlockSpec(memory_space=pltpu.VMEM)
 HBM = pl.BlockSpec(memory_space=pltpu.HBM)
+ANY = pl.BlockSpec(memory_space=pl.ANY)
 SMEM = pl.BlockSpec(memory_space=pltpu.SMEM)
 
 
@@ -29,8 +35,12 @@
     return pltpu.with_memory_space_constraint(array, pltpu.HBM)
 
 
+def in_vmem(array):
+    return pltpu.with_memory_space_constraint(array, pltpu.VMEM)
+
+
 def params():
-    return pltpu.CompilerParams(vmem_limit_bytes=40 << 20)
+    return pltpu.CompilerParams(vmem_limit_bytes=16 << 20)
 
 
 def folded(matrix, perm_row):
@@ -49,42 +59,42 @@
     order_ref,
     s_ref,
     pack_ref,
+    rows_ref,
     t_ref,
-    b_ref,
+    basis_buf,
     coords_ref,
     perm_ref,
     sems,
 ):
+    points = pltpu.make_async_copy(points_ref, coords_ref, sems.at[0])
+    first = pltpu.make_async_copy(transfer_ref.at[0], t_ref.at[0], sems.at[1])
+    order = pltpu.make_async_copy(order_ref, perm_ref, sems.at[2])
     copies = []
     for leaf in range(2):
         block = pl.ds(leaf * LEAF, LEAF)
         copies.append(
             (
-                pltpu.make_async_copy(basis_ref.at[leaf], b_ref.at[leaf], sems.at[2 * leaf]),
-                pltpu.make_async_copy(
-                    x_ref.at[block], pack_ref.at[block], sems.at[2 * leaf + 1]
-                ),
+                pltpu.make_async_copy(basis_ref.at[leaf], basis_buf.at[leaf], sems.at[3 + leaf]),
+                pltpu.make_async_copy(x_ref.at[block], pack_ref.at[block], sems.at[5 + leaf]),
             )
         )
-    points = pltpu.make_async_copy(points_ref, coords_ref, sems.at[4])
-    first = pltpu.make_async_copy(transfer_ref.at[0], t_ref.at[0], sems.at[5])
-    order = pltpu.make_async_copy(order_ref, perm_ref, sems.at[6])
+    points.start()
     for pair in copies:
         for copy in pair:
             copy.start()
-    points.start()
     first.start()
     order.start()
     points.wait()
-    pack_ref[ROWS:, :] = jnp.concatenate(
-        [coords_ref[0], coords_ref[1], jnp.zeros((12, COLS), BF16)], axis=0
-    )
+    rows_ref[...] = jnp.concatenate(
+        [coords_ref[0], coords_ref[1], jnp.zeros((PACK - ROWS - 4, COLS), BF16)], axis=0
+    )
+    pack_ref[ROWS:, :] = rows_ref[...]
     total = None
     for leaf in range(2):
         for copy in copies[leaf]:
             copy.wait()
         part = jnp.dot(
-            b_ref[leaf], pack_ref[leaf * LEAF : (leaf + 1) * LEAF, :], preferred_element_type=F32
+            basis_buf[leaf], pack_ref[leaf * LEAF : (leaf + 1) * LEAF, :], preferred_element_type=F32
         )
         total = part if total is None else total + part
     s_ref[...] = total.astype(BF16)
@@ -99,10 +109,11 @@
         out_shape=(
             jax.ShapeDtypeStruct((RANK, COLS), BF16),
             jax.ShapeDtypeStruct((PACK, COLS), BF16),
+            jax.ShapeDtypeStruct((PACK - ROWS, COLS), BF16),
             jax.ShapeDtypeStruct((1, 2, RANK, RANK), BF16),
         ),
         in_specs=[HBM] * 5,
-        out_specs=(VMEM, VMEM, VMEM),
+        out_specs=(VMEM,) * 4,
         scratch_shapes=[
             pltpu.VMEM((2, RANK, LEAF), BF16),
             pltpu.VMEM((2, 2, LEAF), BF16),
@@ -172,48 +183,98 @@
     )(*args)
 
 
-def near_kernel(index_ref, own_ref, low_ref, high_ref, near_ref):
-    sides = (low_ref, own_ref, high_ref)
-    scale = 1.0 / FACTOR
-    points = own_ref[ROWS : ROWS + 8, :].astype(F32) * scale
-    columns = points.T
-    rows = [side[ROWS : ROWS + 8, :].astype(F32) * scale for side in sides]
+def scaled(rows):
+    return rows.astype(F32) * (1.0 / FACTOR)
+
+
+def add_tile(index_ref, near_ref, target, offset, source, leaf, columns, rows):
+    block = pl.ds(target * LEAF, LEAF)
+    used = (
+        (index_ref[target, 0] == offset)
+        | (index_ref[target, 1] == offset)
+        | (index_ref[target, 2] == offset)
+    )
+
+    @pl.when(used)
+    def _():
+        dx = columns[:, 2 * target : 2 * target + 1] - rows[2 * leaf : 2 * leaf + 1, :]
+        dy = columns[:, 2 * target + 1 : 2 * target + 2] - rows[2 * leaf + 1 : 2 * leaf + 2, :]
+        tile = lax.rsqrt(dx * dx + dy * dy + SOFT / FACTOR**2).astype(BF16)
+        near_ref[block, :] += jnp.dot(
+            tile, source[leaf * LEAF : (leaf + 1) * LEAF, :], preferred_element_type=F32
+        )
+
+
+def own_kernel(index_ref, own_ref, rows_ref, after_ref, near_ref):
+    near_ref[...] = jnp.zeros((ROWS, COLS), F32)
+    rows = scaled(rows_ref[:8, :])
+    columns = rows.T
     for target in range(2):
-        block = pl.ds(target * LEAF, LEAF)
-        near_ref[block, :] = jnp.zeros((LEAF, COLS), F32)
-        tx = columns[:, 2 * target : 2 * target + 1]
-        ty = columns[:, 2 * target + 1 : 2 * target + 2]
-        for offset in (0, 1, -1, 2, -2):
-            side, leaf = divmod(target + offset + 2, 2)
-            used = (
-                (index_ref[target, 0] == offset)
-                | (index_ref[target, 1] == offset)
-                | (index_ref[target, 2] == offset)
-            )
-
-            @pl.when(used)
-            def _(side=side, leaf=leaf, tx=tx, ty=ty, block=block):
-                sx = rows[side][2 * leaf : 2 * leaf + 1, :]
-                sy = rows[side][2 * leaf + 1 : 2 * leaf + 2, :]
-                dx = tx - sx
-                dy = ty - sy
-                tile = lax.rsqrt(dx * dx + dy * dy + SOFT * scale * scale).astype(BF16)
-                near_ref[block, :] += jnp.dot(
-                    tile,
-                    sides[side][leaf * LEAF : (leaf + 1) * LEAF, :],
-                    preferred_element_type=F32,
-                )
-
-
-def near_field(index, own, low, high):
-    return pl.pallas_call(
-        near_kernel,
+        for leaf in range(2):
+            add_tile(index_ref, near_ref, target, leaf - target, own_ref, leaf, columns, rows)
+
+
+def near_own(index, own, rows, after):
+    return pl.pallas_call(
+        own_kernel,
         out_shape=jax.ShapeDtypeStruct((ROWS, COLS), F32),
         in_specs=[SMEM, VMEM, VMEM, VMEM],
         out_specs=VMEM,
         compiler_params=params(),
-        name="near",
-    )(index, own, low, high)
+        name="near_own",
+    )(index, own, rows, after)
+
+
+def sides_kernel(tests, index_ref, wide_ref, pair_ref, rows_ref, *refs):
+    count = len(tests)
+    sources = refs[:count]
+    near_ref = refs[count + 1]
+    bufs, sems = refs[count + 2 : -1], refs[-1]
+    plan = []
+    for i, test in enumerate(tests):
+        low, high = test(wide_ref[0], pair_ref[0])
+        copy = pltpu.make_async_copy(sources[i], bufs[i], sems.at[i])
+        plan.append((low, high, copy, bufs[i]))
+
+        @pl.when(low | high)
+        def _(copy=copy):
+            copy.start()
+
+    for low, high, copy, buf in plan:
+
+        @pl.when(low | high)
+        def _(copy=copy):
+            copy.wait()
+
+        for shift, present in ((-2, low), (2, high)):
+
+            @pl.when(present)
+            def _(shift=shift, buf=buf):
+                columns = scaled(rows_ref[:8, :]).T
+                rows = scaled(buf[ROWS : ROWS + 8, :])
+                for target in range(2):
+                    for leaf in range(2):
+                        offset = shift + leaf - target
+                        if abs(offset) <= 2:
+                            add_tile(index_ref, near_ref, target, offset, buf, leaf, columns, rows)
+
+
+def near_sides(name, weight, index, place, rows, tests, sources, near):
+    count = len(tests)
+    return pl.pallas_call(
+        functools.partial(sides_kernel, tests),
+        out_shape=jax.ShapeDtypeStruct((ROWS, COLS), F32),
+        in_specs=[SMEM] * 3 + [VMEM] + [ANY] * count + [VMEM],
+        out_specs=VMEM,
+        scratch_shapes=[pltpu.VMEM((PACK, COLS), BF16)] * count
+        + [pltpu.SemaphoreType.DMA((count,))],
+        input_output_aliases={4 + count: 0},
+        compiler_params=params(),
+        cost_estimate=pl.CostEstimate(
+            flops=weight, transcendentals=0, bytes_accessed=ROWS * COLS * 8
+        ),
+        name=name,
+    )(index, *place, rows, *sources, near)
 
 
 def final_kernel(t_ref, own_ref, other_ref, e_ref, near_ref, out_ref, s_ref):
@@ -262,25 +323,66 @@
 
 def on_device(rhs, coords, near_index, project_basis, expand_basis, transfer, level_perm):
     axes = ("wide", "pair")
-    devices = lax.axis_size("wide") * lax.axis_size("pair")
-    up = [(i, i + 1) for i in range(devices - 1)]
-    down = [(i + 1, i) for i in range(devices - 1)]
-    s, pack, t0 = project(
+    wide, pair = lax.axis_size("wide"), lax.axis_size("pair")
+    devices = wide * pair
+    turn = 4 * pair
+
+    def odd(i):
+        return i % 2 == 1
+
+    def even(i):
+        return (i % 2 == 0) & (i % RUN != 0)
+
+    def outer(i):
+        return (i % RUN == 0) & (i % turn != 0)
+
+    def far(i):
+        return i % turn == 0
+
+    def swapped(block, keep):
+        up = [(i - 1, i) for i in range(1, devices) if keep(i)]
+        return lax.ppermute(block, axes, up + [(b, a) for a, b in up])
+
+    def met(keep):
+        def test(w, q):
+            i = w * pair + q
+            return keep(i) & (i > 0), keep(i + 1) & (i + 1 < devices)
+
+        return test
+
+    place = (lax.axis_index("wide").reshape(1), lax.axis_index("pair").reshape(1))
+    s, pack, rows, t0 = project(
         rhs, jnp.swapaxes(project_basis, 1, 2), coords, transfer[0], level_perm
     )
+    odd_side = swapped(pack, odd)
+    even_side = swapped(pack, even)
     both, high_bit = with_partner(s, "wide", 0)
     s = level_step(t0, 0, s, both, high_bit)
     partner = from_partner(s, "wide", 1)
     t, e = prepare(transfer[0], level_perm, jnp.swapaxes(expand_basis, 1, 2), s)
     sent, e = lax.optimization_barrier((pack, e))
-    low = lax.ppermute(sent, axes, up)
-    high = lax.ppermute(sent, axes, down)
-    s = level_step(t, 0, s, partner, weight=COVER)
-    s = level_step(t, 1, s, from_partner(s, "wide", 2))
+    outer_side = swapped(sent, outer)
+    s = level_step(t, 0, s, partner, weight=COVER_1)
+    partner = from_partner(s, "wide", 2)
+    sent, s = lax.optimization_barrier((sent, s))
+    far_side = swapped(sent, far)
+    near = near_own(near_index, sent, rows, s)
+    partner, near = lax.optimization_barrier((partner, near))
+    s = level_step(t, 1, s, partner)
     both, high_bit = with_partner(s, "pair", 0)
     s = level_step(t, 2, s, both, high_bit)
     partner = from_partner(s, "pair", 1)
-    near = near_field(near_index, pack, low, high)
+
+    def add(name, weight, near, *sides):
+        tests = [met(keep) for keep, _ in sides]
+        sources = [side for _, side in sides]
+        return near_sides(name, weight, near_index, place, rows, tests, sources, near)
+
+    near = add(
+        "near_inner", COVER_INNER, near, (odd, in_hbm(odd_side)), (even, in_hbm(even_side))
+    )
+    near = add("near_outer", COVER_OUTER, near, (outer, outer_side))
+    near = add("near_far", COVER_FAR, near, (far, far_side))
     return final_step(t, s, partner, e, near)
 
 

time: 67.8 us -> 58.1 us (0.86)
  the two profiles are of different devices: /device:TPU:16 before, /device:TPU:1 now
where the time goes in v3:
time: 58.1 us; the launch traced here: 57.7 us
  starting transfers between devices  23.5 us (40%)
  Pallas kernels  14.5 us (25%)
  blocking collectives  12.9 us (22%)
  waiting for transfers between devices  5.46 us (9%)
  local copies, waits for them, and re-layouts  1.01 us (2%)
    ppermute x4, starting transfers between devices, swapped(): return lax.ppermute(block, axes, up + [(b, a) for a, b in up])  16.5 us
    all_gather x2, blocking collectives, with_partner(): both = lax.all_gather(block, axis, axis_index_groups=pairs)  12.9 us
    ppermute x3, starting transfers between devices, from_partner(): return lax.ppermute(block, axis, [(i, i ^ 1 << bit) for i in range(count)])  7.05 us
    pallas_call x3, Pallas kernels, near_sides(): pl.pallas_call(functools.partial(sides_kernel, tests), out_shape=jax.Shap...  6.97 us
    ppermute x4, waiting for transfers between devices, swapped(): return lax.ppermute(block, axes, up + [(b, a) for a, b in up])  3.01 us
    ppermute x3, waiting for transfers between devices, from_partner(): return lax.ppermute(block, axis, [(i, i ^ 1 << bit) for i in range(count)])  2.45 us
    pallas_call x1, Pallas kernels, final_step(): pl.pallas_call(final_kernel, grid=(ROWS // block,), out_shape=jax.ShapeDt...  2.34 us
    pallas_call x1, Pallas kernels, project(): pl.pallas_call(project_kernel, out_shape=(jax.ShapeDtypeStruct((RANK, COL...  2.02 us
  transfers between devices with their start and end apart: 7, of which 3 were waited for; matrix products, arithmetic and copies ran while one was open for 0% of the time, Pallas kernels for 18%

profile of v3, /device:TPU:1, one launch (start us, length us, event | category | flops | bytes accessed | tf_op | source)
XLA Modules:
  0.0 57.7 jit_solution(10065907190905542970)
XLA Ops:
  0.0 2.0 %project.1 = (bf16[192,512]{1,0:T(8,128)(2,1)S(1)}, bf16[1040,512]{1,0:T(8,128)(2,1)S(1)}, bf16[16,512]{1,0:T(8,128)(2,1)S(1)}, bf16[1,2,192,192]{3,2,1,0:T(8,128)(2,1)S(1)}) custom-call(bf16[1024,512]{1,0:T(8,128)(2,1)} %x_ref.1, bf16[2,192,512]{2,1,0:T(8,128)(2,1)} %bitcast.14, bf16[2,2,512]{2,1,0:T(2,128)(2,1)} %points_ref.1, ...), custom_call_target="tpu_custom_call" | custom-call | tf_op jit(solution)/shard_map/project/pallas_call | solution.py:107
  2.0 5.0 %collective-permute-start.5 = (bf16[1040,512]{1,0:T(8,128)(2,1)S(1)}, bf16[1040,512]{1,0:T(8,128)(2,1)}, u32[]{:S(2)}, u32[]{:S(2)}) collective-permute-start(bf16[1040,512]{1,0:T(8,128)(2,1)S(1)} %get-tuple-element.24.own_ref), channel_id=1, source_target_pairs={{0,1},{2,3},{4,5},{6,7},{8,9},{10,11},{12,13},{14,15},{16,17},{18,... | collective-permute-start | bytes 3194888 | tf_op jit(solution)/shard_map/ppermute | solution.py:344
  7.0 1.7 %collective-permute-start.6 = (bf16[1040,512]{1,0:T(8,128)(2,1)S(1)}, bf16[1040,512]{1,0:T(8,128)(2,1)}, u32[]{:S(2)}, u32[]{:S(2)}) collective-permute-start(bf16[1040,512]{1,0:T(8,128)(2,1)S(1)} %get-tuple-element.24.own_ref), channel_id=1, source_target_pairs={{1,2},{3,4},{5,6},{9,10},{11,12},{13,14},{17,18},{19,20},{21,22},{... | collective-permute-start | bytes 3194888 | tf_op jit(solution)/shard_map/ppermute | solution.py:344
  8.7 5.7 %all-gather = bf16[384,512]{1,0:T(8,128)(2,1)S(1)} all-gather(bf16[192,512]{1,0:T(8,128)(2,1)S(1)} %get-tuple-element.18.own_ref), channel_id=2, replica_groups={{0,16},{32,48},{64,80},{96,112},{128,144},{160,176},{192,208},{224,240}..., dimensions={0}, use_global_device_ids=true | all-gather | bytes 589824 | tf_op jit(solution)/shard_map/all_gather | solution.py:319
  14.4 0.2 level_0.2.after_ref.own_ref
  14.6 1.9 %collective-permute-start = (bf16[192,512]{1,0:T(8,128)(2,1)S(1)}, bf16[192,512]{1,0:T(8,128)(2,1)S(1)}, u32[]{:S(2)}, u32[]{:S(2)}) collective-permute-start(bf16[192,512]{1,0:T(8,128)(2,1)S(1)} %level_0.2.after_ref.own_ref), channel_id=1, source_target_pairs={{0,32},{16,48},{32,0},{48,16},{64,96},{80,112},{96,64},{112,80},{1... | collective-permute-start | bytes 589832 | tf_op jit(solution)/shard_map/ppermute | solution.py:313
  16.6 1.0 %copy-done.1 = bf16[2,512,192]{1,2,0:T(8,128)(2,1)S(1)} copy-done((bf16[2,512,192]{1,2,0:T(8,128)(2,1)S(1)}, bf16[2,512,192]{1,2,0:T(8,128)(2,1)}, u32[]{:S(2)}) %copy-start.1) | copy-done | bytes 393240
  17.6 0.4 prepare.1
  18.0 9.1 %collective-permute-start.4 = (bf16[1040,512]{1,0:T(8,128)(2,1)S(1)}, bf16[1040,512]{1,0:T(8,128)(2,1)}, u32[]{:S(2)}, u32[]{:S(2)}) collective-permute-start(bf16[1040,512]{1,0:T(8,128)(2,1)S(1)} %get-tuple-element.24.own_ref), channel_id=1, source_target_pairs={{7,8},{15,16},{23,24},{31,32},{39,40},{47,48},{55,56},{71,72},{79,... | collective-permute-start | bytes 3194888 | tf_op jit(solution)/shard_map/ppermute | solution.py:344
  27.1 0.2 level_0.3.after_ref.own_ref
  27.4 3.2 %collective-permute-start.1 = (bf16[192,512]{1,0:T(8,128)(2,1)S(1)}, bf16[192,512]{1,0:T(8,128)(2,1)S(1)}, u32[]{:S(2)}, u32[]{:S(2)}) collective-permute-start(bf16[192,512]{1,0:T(8,128)(2,1)S(1)} %level_0.3.after_ref.own_ref), channel_id=1, source_target_pairs={{0,64},{16,80},{32,96},{48,112},{64,0},{80,16},{96,32},{112,48},{1... | collective-permute-start | bytes 589832 | tf_op jit(solution)/shard_map/ppermute | solution.py:313
  30.6 0.7 %collective-permute-start.3 = (bf16[1040,512]{1,0:T(8,128)(2,1)S(1)}, bf16[1040,512]{1,0:T(8,128)(2,1)S(1)}, u32[]{:S(2)}, u32[]{:S(2)}) collective-permute-start(bf16[1040,512]{1,0:T(8,128)(2,1)S(1)} %get-tuple-element.24.own_ref), channel_id=1, source_target_pairs={{63,64},{127,128},{191,192},{255,256},{319,320},{383,384},{447,448... | collective-permute-start | bytes 3194888 | tf_op jit(solution)/shard_map/ppermute | solution.py:344
  31.3 1.9 %near_own.1.refs_2_ = f32[1024,512]{1,0:T(8,128)S(1)} custom-call(s32[2,3]{1,0:T(2,128)S(1)} %copy-done.3, bf16[1040,512]{1,0:T(8,128)(2,1)S(1)} %get-tuple-element.24.own_ref, bf16[16,512]{1,0:T(8,128)(2,1)S(1)} %get-tuple-element.25.rows_ref, bf16[192,512]{1,0:T(8,128)(2,1)S(1)} %level_0.3.after_ref.own_ref), custom_call_target="tpu_custom_call" | custom-call | tf_op jit(solution)/shard_map/near_own/pallas_call | solution.py:218
  33.2 1.4 %collective-permute-done.1.other_ref = bf16[192,512]{1,0:T(8,128)(2,1)S(1)} collective-permute-done((bf16[192,512]{1,0:T(8,128)(2,1)S(1)}, bf16[192,512]{1,0:T(8,128)(2,1)S(1)}, u32[]{:S(2)}, u32[]{:S(2)}) %collective-permute-start.1) | collective-permute-done | bytes 196640 | tf_op jit(solution)/shard_map/ppermute | solution.py:313
  34.6 0.2 level_1.1.own_ref
  34.9 7.2 %all-gather.1 = bf16[384,512]{1,0:T(8,128)(2,1)S(1)} all-gather(bf16[192,512]{1,0:T(8,128)(2,1)S(1)} %level_1.1.own_ref), channel_id=3, replica_groups={{0,1},{2,3},{4,5},{6,7},{8,9},{10,11},{12,13},{14,15},{16,17},{18,19},{..., dimensions={0}, use_global_device_ids=true | all-gather | bytes 589824 | tf_op jit(solution)/shard_map/all_gather | solution.py:319
  42.1 0.2 level_2.1.own_ref
  42.3 1.9 %collective-permute-start.2 = (bf16[192,512]{1,0:T(8,128)(2,1)S(1)}, bf16[192,512]{1,0:T(8,128)(2,1)S(1)}, u32[]{:S(2)}, u32[]{:S(2)}) collective-permute-start(bf16[192,512]{1,0:T(8,128)(2,1)S(1)} %level_2.1.own_ref), channel_id=1, source_target_pairs={{0,2},{1,3},{2,0},{3,1},{4,6},{5,7},{6,4},{7,5},{8,10},{9,11},{10,... | collective-permute-start | bytes 589832 | tf_op jit(solution)/shard_map/ppermute | solution.py:313
  44.3 3.1 %near_inner.1.refs_1_ = f32[1024,512]{1,0:T(8,128)S(1)} custom-call(s32[2,3]{1,0:T(2,128)S(1)} %copy-done.3, s32[1]{0:T(128)} %bitcast.7.wide_ref, s32[1]{0:T(128)} %bitcast.8.pair_ref, bf16[16,512]{1,0:T(8,128)(2,1)S(1)} %get-tuple-element.25.rows_ref, bf16[1040,512]{1,0:T(8,128)(2,1)} %collective-permute-done.5.refs_0_, ...), custom_call_target="tpu_custom_call", output_to_operand_aliasing={{}: (6, {})} | custom-call | flops 5000000000 | bytes 4194304 | tf_op jit(solution)/shard_map/near_inner/pallas_call | solution.py:264
  47.4 3.0 %collective-permute-done.4.refs_0_ = bf16[1040,512]{1,0:T(8,128)(2,1)} collective-permute-done((bf16[1040,512]{1,0:T(8,128)(2,1)S(1)}, bf16[1040,512]{1,0:T(8,128)(2,1)}, u32[]{:S(2)}, u32[]{:S(2)}) %collective-permute-start.4) | collective-permute-done | bytes 1064992 | tf_op jit(solution)/shard_map/ppermute | solution.py:344
  50.4 3.3 %near_outer.1.refs_1_ = f32[1024,512]{1,0:T(8,128)S(1)} custom-call(s32[2,3]{1,0:T(2,128)S(1)} %copy-done.3, s32[1]{0:T(128)} %bitcast.7.wide_ref, s32[1]{0:T(128)} %bitcast.8.pair_ref, bf16[16,512]{1,0:T(8,128)(2,1)S(1)} %get-tuple-element.25.rows_ref, bf16[1040,512]{1,0:T(8,128)(2,1)} %collective-permute-done.4.refs_0_, ...), custom_call_target="tpu_custom_call", output_to_operand_aliasing={{}: (5, {})} | custom-call | flops 6000000000 | bytes 4194304 | tf_op jit(solution)/shard_map/near_outer/pallas_call | solution.py:264
  53.7 0.6 %near_far.1.near_ref = f32[1024,512]{1,0:T(8,128)S(1)} custom-call(s32[2,3]{1,0:T(2,128)S(1)} %copy-done.3, s32[1]{0:T(128)} %bitcast.7.wide_ref, s32[1]{0:T(128)} %bitcast.8.pair_ref, bf16[16,512]{1,0:T(8,128)(2,1)S(1)} %get-tuple-element.25.rows_ref, bf16[1040,512]{1,0:T(8,128)(2,1)S(1)} %collective-permute-done.3.refs_0_, ...), custom_call_target="tpu_custom_call", output_to_operand_aliasing={{}: (5, {})} | custom-call | flops 4000000000 | bytes 4194304 | tf_op jit(solution)/shard_map/near_far/pallas_call | solution.py:264
  54.3 1.1 %collective-permute-done.2.other_ref = bf16[192,512]{1,0:T(8,128)(2,1)S(1)} collective-permute-done((bf16[192,512]{1,0:T(8,128)(2,1)S(1)}, bf16[192,512]{1,0:T(8,128)(2,1)S(1)}, u32[]{:S(2)}, u32[]{:S(2)}) %collective-permute-start.2) | collective-permute-done | bytes 196640 | tf_op jit(solution)/shard_map/ppermute | solution.py:313
  55.4 2.3 %final.1 = bf16[1024,512]{1,0:T(8,128)(2,1)} custom-call(bf16[4,2,192,192]{3,2,1,0:T(8,128)(2,1)S(1)} %get-tuple-element.19.t_ref, bf16[192,512]{1,0:T(8,128)(2,1)S(1)} %level_2.1.own_ref, bf16[192,512]{1,0:T(8,128)(2,1)S(1)} %collective-permute-done.2.other_ref, bf16[1024,192]{1,0:T(8,128)(2,1)S(1)} %get-tuple-element.27.e_ref, ...), custom_call_target="tpu_custom_call" | custom-call | tf_op jit(solution)/shard_map/final/pallas_call | solution.py:293
  (11 shorter events, 0.0 us)
Async XLA Ops:
  2.0 14.5 %copy-start = (bf16[1,5,2,192,192]{4,3,2,1,0:T(8,128)(2,1)S(1)}, bf16[1,5,2,192,192]{4,3,2,1,0:T(8,128)(2,1)}, u32[]{:S(2)}) copy-start(bf16[1,5,2,192,192]{4,3,2,1,0:T(8,128)(2,1)} %param.12) | copy-start | bytes 2211844
  2.0 14.5 %copy-start.2 = (s32[5,192]{1,0:T(8,128)S(1)}, s32[5,192]{1,0:T(8,128)}, u32[]{:S(2)}) copy-start(s32[5,192]{1,0:T(8,128)} %perm_ref.1) | copy-start | bytes 11524
  2.0 42.2 %collective-permute-start.5 = (bf16[1040,512]{1,0:T(8,128)(2,1)S(1)}, bf16[1040,512]{1,0:T(8,128)(2,1)}, u32[]{:S(2)}, u32[]{:S(2)}) collective-permute-start(bf16[1040,512]{1,0:T(8,128)(2,1)S(1)} %get-tuple-element.24.own_ref), channel_id=1, source_target_pairs={{0,1},{2,3},{4,5},{6,7},{8,9},{10,11},{12,13},{14,15},{16,17},{18,... | collective-permute-start | bytes 3194888 | tf_op jit(solution)/shard_map/ppermute | solution.py:344
  7.0 37.3 %collective-permute-start.6 = (bf16[1040,512]{1,0:T(8,128)(2,1)S(1)}, bf16[1040,512]{1,0:T(8,128)(2,1)}, u32[]{:S(2)}, u32[]{:S(2)}) collective-permute-start(bf16[1040,512]{1,0:T(8,128)(2,1)S(1)} %get-tuple-element.24.own_ref), channel_id=1, source_target_pairs={{1,2},{3,4},{5,6},{9,10},{11,12},{13,14},{17,18},{19,20},{21,22},{... | collective-permute-start | bytes 3194888 | tf_op jit(solution)/shard_map/ppermute | solution.py:344
  14.6 12.4 %collective-permute-start = (bf16[192,512]{1,0:T(8,128)(2,1)S(1)}, bf16[192,512]{1,0:T(8,128)(2,1)S(1)}, u32[]{:S(2)}, u32[]{:S(2)}) collective-permute-start(bf16[192,512]{1,0:T(8,128)(2,1)S(1)} %level_0.2.after_ref.own_ref), channel_id=1, source_target_pairs={{0,32},{16,48},{32,0},{48,16},{64,96},{80,112},{96,64},{112,80},{1... | collective-permute-start | bytes 589832 | tf_op jit(solution)/shard_map/ppermute | solution.py:313
  16.6 1.0 %copy-start.1 = (bf16[2,512,192]{1,2,0:T(8,128)(2,1)S(1)}, bf16[2,512,192]{1,2,0:T(8,128)(2,1)}, u32[]{:S(2)}) copy-start(bf16[2,512,192]{1,2,0:T(8,128)(2,1)} %param.11) | copy-start | bytes 1179652
  18.0 32.5 %collective-permute-start.4 = (bf16[1040,512]{1,0:T(8,128)(2,1)S(1)}, bf16[1040,512]{1,0:T(8,128)(2,1)}, u32[]{:S(2)}, u32[]{:S(2)}) collective-permute-start(bf16[1040,512]{1,0:T(8,128)(2,1)S(1)} %get-tuple-element.24.own_ref), channel_id=1, source_target_pairs={{7,8},{15,16},{23,24},{31,32},{39,40},{47,48},{55,56},{71,72},{79,... | collective-permute-start | bytes 3194888 | tf_op jit(solution)/shard_map/ppermute | solution.py:344
  27.1 4.2 %copy-start.3 = (s32[2,3]{1,0:T(2,128)S(1)}, s32[2,3]{1,0:T(2,128)}, u32[]{:S(2)}) copy-start(s32[2,3]{1,0:T(2,128)} %index_ref.7) | copy-start | bytes 76
  27.4 7.2 %collective-permute-start.1 = (bf16[192,512]{1,0:T(8,128)(2,1)S(1)}, bf16[192,512]{1,0:T(8,128)(2,1)S(1)}, u32[]{:S(2)}, u32[]{:S(2)}) collective-permute-start(bf16[192,512]{1,0:T(8,128)(2,1)S(1)} %level_0.3.after_ref.own_ref), channel_id=1, source_target_pairs={{0,64},{16,80},{32,96},{48,112},{64,0},{80,16},{96,32},{112,48},{1... | collective-permute-start | bytes 589832 | tf_op jit(solution)/shard_map/ppermute | solution.py:313
  30.6 23.1 %collective-permute-start.3 = (bf16[1040,512]{1,0:T(8,128)(2,1)S(1)}, bf16[1040,512]{1,0:T(8,128)(2,1)S(1)}, u32[]{:S(2)}, u32[]{:S(2)}) collective-permute-start(bf16[1040,512]{1,0:T(8,128)(2,1)S(1)} %get-tuple-element.24.own_ref), channel_id=1, source_target_pairs={{63,64},{127,128},{191,192},{255,256},{319,320},{383,384},{447,448... | collective-permute-start | bytes 3194888 | tf_op jit(solution)/shard_map/ppermute | solution.py:344
  42.3 13.0 %collective-permute-start.2 = (bf16[192,512]{1,0:T(8,128)(2,1)S(1)}, bf16[192,512]{1,0:T(8,128)(2,1)S(1)}, u32[]{:S(2)}, u32[]{:S(2)}) collective-permute-start(bf16[192,512]{1,0:T(8,128)(2,1)S(1)} %level_2.1.own_ref), channel_id=1, source_target_pairs={{0,2},{1,3},{2,0},{3,1},{4,6},{5,7},{6,4},{7,5},{8,10},{9,11},{10,... | collective-permute-start | bytes 589832 | tf_op jit(solution)/shard_map/ppermute | solution.py:313

commit v4 on v3

--- a/solution.py
+++ b/solution.py
@@ -17,8 +17,11 @@
 ROWS = 1024
 PACK = ROWS + 16
 RUN = 8
+CHUNK = 128
+PIECE = 128
 COVER_1 = 3_000_000_000
-COVER_INNER = 5_000_000_000
+COVER_ODD = 3_500_000_000
+COVER_EVEN = 1_000_000_000
 COVER_OUTER = 6_000_000_000
 COVER_FAR = 4_000_000_000
 SOFT = 0.0004
@@ -33,10 +36,6 @@
 
 def in_hbm(array):
     return pltpu.with_memory_space_constraint(array, pltpu.HBM)
-
-
-def in_vmem(array):
-    return pltpu.with_memory_space_constraint(array, pltpu.VMEM)
 
 
 def params():
@@ -125,26 +124,21 @@
     )(*(in_hbm(array) for array in (x, basis_t, coords, transfer, perm)))
 
 
-def prepare_kernel(transfer_ref, perm_ref, expand_ref, after_ref, t_ref, e_ref):
+def prepare_kernel(transfer_ref, perm_ref, after_ref, t_ref):
     for level in range(1, LEVELS):
         t_ref[level - 1, 0] = transfer_ref[level, 0]
         t_ref[level - 1, 1] = folded(transfer_ref[level, 1], perm_ref[level : level + 1, :])
-    for leaf in range(2):
-        e_ref[leaf * LEAF : (leaf + 1) * LEAF, :] = expand_ref[leaf].T
-
-
-def prepare(transfer, perm, expand_t, after):
+
+
+def prepare(transfer, perm, after):
     return pl.pallas_call(
         prepare_kernel,
-        out_shape=(
-            jax.ShapeDtypeStruct((LEVELS - 1, 2, RANK, RANK), BF16),
-            jax.ShapeDtypeStruct((ROWS, RANK), BF16),
-        ),
-        in_specs=[VMEM, VMEM, VMEM, VMEM],
-        out_specs=(VMEM, VMEM),
+        out_shape=jax.ShapeDtypeStruct((LEVELS - 1, 2, RANK, RANK), BF16),
+        in_specs=[VMEM, VMEM, VMEM],
+        out_specs=VMEM,
         compiler_params=params(),
         name="prepare",
-    )(transfer, perm, expand_t, after)
+    )(transfer, perm, after)
 
 
 def level_kernel(t_ref, own_ref, other_ref, s_ref):
@@ -188,7 +182,6 @@
 
 
 def add_tile(index_ref, near_ref, target, offset, source, leaf, columns, rows):
-    block = pl.ds(target * LEAF, LEAF)
     used = (
         (index_ref[target, 0] == offset)
         | (index_ref[target, 1] == offset)
@@ -197,15 +190,22 @@
 
     @pl.when(used)
     def _():
-        dx = columns[:, 2 * target : 2 * target + 1] - rows[2 * leaf : 2 * leaf + 1, :]
-        dy = columns[:, 2 * target + 1 : 2 * target + 2] - rows[2 * leaf + 1 : 2 * leaf + 2, :]
-        tile = lax.rsqrt(dx * dx + dy * dy + SOFT / FACTOR**2).astype(BF16)
-        near_ref[block, :] += jnp.dot(
-            tile, source[leaf * LEAF : (leaf + 1) * LEAF, :], preferred_element_type=F32
-        )
-
-
-def own_kernel(index_ref, own_ref, rows_ref, after_ref, near_ref):
+        sx = rows[2 * leaf : 2 * leaf + 1, :]
+        sy = rows[2 * leaf + 1 : 2 * leaf + 2, :]
+        held = source[leaf * LEAF : (leaf + 1) * LEAF, :]
+        for start in range(0, LEAF, PIECE):
+            part = columns[start : start + PIECE]
+            dx = part[:, 2 * target : 2 * target + 1] - sx
+            dy = part[:, 2 * target + 1 : 2 * target + 2] - sy
+            tile = lax.rsqrt(dx * dx + dy * dy + SOFT / FACTOR**2).astype(BF16)
+            near_ref[pl.ds(target * LEAF + start, PIECE), :] += jnp.dot(
+                tile, held, preferred_element_type=F32
+            )
+
+
+def own_kernel(index_ref, own_ref, rows_ref, expand_ref, after_ref, near_ref, e_ref):
+    for leaf in range(2):
+        e_ref[leaf * LEAF : (leaf + 1) * LEAF, :] = expand_ref[leaf].T
     near_ref[...] = jnp.zeros((ROWS, COLS), F32)
     rows = scaled(rows_ref[:8, :])
     columns = rows.T
@@ -214,95 +214,91 @@
             add_tile(index_ref, near_ref, target, leaf - target, own_ref, leaf, columns, rows)
 
 
-def near_own(index, own, rows, after):
+def near_own(index, own, rows, expand_t, after):
     return pl.pallas_call(
         own_kernel,
+        out_shape=(
+            jax.ShapeDtypeStruct((ROWS, COLS), F32),
+            jax.ShapeDtypeStruct((ROWS, RANK), BF16),
+        ),
+        in_specs=[SMEM] + [VMEM] * 4,
+        out_specs=(VMEM, VMEM),
+        compiler_params=params(),
+        name="near_own",
+    )(index, own, rows, expand_t, after)
+
+
+def side_kernel(
+    test, index_ref, wide_ref, pair_ref, rows_ref, source_ref, _, near_ref, buf, sems
+):
+    low, high = test(wide_ref[0], pair_ref[0])
+    spans = ((ROWS, PACK - ROWS), (0, LEAF), (LEAF, LEAF))
+    copies = []
+    for i, (start, size) in enumerate(spans):
+        block = pl.ds(start, size)
+        copies.append(pltpu.make_async_copy(source_ref.at[block], buf.at[block], sems.at[i]))
+
+    @pl.when(low | high)
+    def _():
+        for copy in copies:
+            copy.start()
+
+    for shift, present in ((-2, low), (2, high)):
+
+        @pl.when(present)
+        def _(shift=shift):
+            copies[0].wait()
+            columns = scaled(rows_ref[:8, :]).T
+            rows = scaled(buf[ROWS : ROWS + 8, :])
+            for leaf in range(2):
+                copies[1 + leaf].wait()
+                for target in range(2):
+                    offset = shift + leaf - target
+                    if abs(offset) <= 2:
+                        add_tile(index_ref, near_ref, target, offset, buf, leaf, columns, rows)
+
+
+def near_side(name, weight, index, place, rows, test, source, near):
+    return pl.pallas_call(
+        functools.partial(side_kernel, test),
         out_shape=jax.ShapeDtypeStruct((ROWS, COLS), F32),
-        in_specs=[SMEM, VMEM, VMEM, VMEM],
+        in_specs=[SMEM] * 3 + [VMEM, ANY, VMEM],
         out_specs=VMEM,
-        compiler_params=params(),
-        name="near_own",
-    )(index, own, rows, after)
-
-
-def sides_kernel(tests, index_ref, wide_ref, pair_ref, rows_ref, *refs):
-    count = len(tests)
-    sources = refs[:count]
-    near_ref = refs[count + 1]
-    bufs, sems = refs[count + 2 : -1], refs[-1]
-    plan = []
-    for i, test in enumerate(tests):
-        low, high = test(wide_ref[0], pair_ref[0])
-        copy = pltpu.make_async_copy(sources[i], bufs[i], sems.at[i])
-        plan.append((low, high, copy, bufs[i]))
-
-        @pl.when(low | high)
-        def _(copy=copy):
-            copy.start()
-
-    for low, high, copy, buf in plan:
-
-        @pl.when(low | high)
-        def _(copy=copy):
-            copy.wait()
-
-        for shift, present in ((-2, low), (2, high)):
-
-            @pl.when(present)
-            def _(shift=shift, buf=buf):
-                columns = scaled(rows_ref[:8, :]).T
-                rows = scaled(buf[ROWS : ROWS + 8, :])
-                for target in range(2):
-                    for leaf in range(2):
-                        offset = shift + leaf - target
-                        if abs(offset) <= 2:
-                            add_tile(index_ref, near_ref, target, offset, buf, leaf, columns, rows)
-
-
-def near_sides(name, weight, index, place, rows, tests, sources, near):
-    count = len(tests)
-    return pl.pallas_call(
-        functools.partial(sides_kernel, tests),
-        out_shape=jax.ShapeDtypeStruct((ROWS, COLS), F32),
-        in_specs=[SMEM] * 3 + [VMEM] + [ANY] * count + [VMEM],
-        out_specs=VMEM,
-        scratch_shapes=[pltpu.VMEM((PACK, COLS), BF16)] * count
-        + [pltpu.SemaphoreType.DMA((count,))],
-        input_output_aliases={4 + count: 0},
+        scratch_shapes=[pltpu.VMEM((PACK, COLS), BF16), pltpu.SemaphoreType.DMA((3,))],
+        input_output_aliases={5: 0},
         compiler_params=params(),
         cost_estimate=pl.CostEstimate(
             flops=weight, transcendentals=0, bytes_accessed=ROWS * COLS * 8
         ),
         name=name,
-    )(index, *place, rows, *sources, near)
-
-
-def final_kernel(t_ref, own_ref, other_ref, e_ref, near_ref, out_ref, s_ref):
-    @pl.when(pl.program_id(0) == 0)
-    def _():
-        total = jnp.dot(t_ref[0, 0], own_ref[...], preferred_element_type=F32)
-        total = total + jnp.dot(t_ref[0, 1], other_ref[...], preferred_element_type=F32)
-        s_ref[...] = total.astype(BF16)
-
-    distant = jnp.dot(e_ref[...], s_ref[...], preferred_element_type=F32)
-    out_ref[...] = (near_ref[...] + distant).astype(BF16)
+    )(index, *place, rows, source, near)
+
+
+def final_kernel(t_ref, own_ref, other_ref, e_ref, near_ref, out_ref, out_buf, sems):
+    total = jnp.dot(t_ref[LEVELS - 2, 0], own_ref[...], preferred_element_type=F32)
+    total = total + jnp.dot(t_ref[LEVELS - 2, 1], other_ref[...], preferred_element_type=F32)
+    s = total.astype(BF16)
+    copies = []
+    for i in range(ROWS // CHUNK):
+        block = pl.ds(i * CHUNK, CHUNK)
+        distant = jnp.dot(e_ref[block, :], s, preferred_element_type=F32)
+        out_buf[block, :] = (near_ref[block, :] + distant).astype(BF16)
+        copies.append(pltpu.make_async_copy(out_buf.at[block], out_ref.at[block], sems.at[i]))
+        copies[-1].start()
+    for copy in copies:
+        copy.wait()
 
 
 def final_step(t, own, other, e, near):
-    block = 256
     return pl.pallas_call(
         final_kernel,
-        grid=(ROWS // block,),
         out_shape=jax.ShapeDtypeStruct((ROWS, COLS), BF16),
-        in_specs=[
-            pl.BlockSpec((1, 2, RANK, RANK), lambda i: (LEVELS - 2, 0, 0, 0)),
-            pl.BlockSpec((RANK, COLS), lambda i: (0, 0)),
-            pl.BlockSpec((RANK, COLS), lambda i: (0, 0)),
-            pl.BlockSpec((block, RANK), lambda i: (i, 0)),
-            pl.BlockSpec((block, COLS), lambda i: (i, 0)),
+        in_specs=[VMEM] * 5,
+        out_specs=HBM,
+        scratch_shapes=[
+            pltpu.VMEM((ROWS, COLS), BF16),
+            pltpu.SemaphoreType.DMA((ROWS // CHUNK,)),
         ],
-        out_specs=pl.BlockSpec((block, COLS), lambda i: (i, 0)),
-        scratch_shapes=[pltpu.VMEM((RANK, COLS), BF16)],
         compiler_params=params(),
         name="final",
     )(t, own, other, e, near)
@@ -355,34 +351,31 @@
         rhs, jnp.swapaxes(project_basis, 1, 2), coords, transfer[0], level_perm
     )
     odd_side = swapped(pack, odd)
-    even_side = swapped(pack, even)
     both, high_bit = with_partner(s, "wide", 0)
     s = level_step(t0, 0, s, both, high_bit)
     partner = from_partner(s, "wide", 1)
-    t, e = prepare(transfer[0], level_perm, jnp.swapaxes(expand_basis, 1, 2), s)
-    sent, e = lax.optimization_barrier((pack, e))
+    sent, s = lax.optimization_barrier((pack, s))
     outer_side = swapped(sent, outer)
+    even_side = swapped(sent, even)
+    t = prepare(transfer[0], level_perm, s)
     s = level_step(t, 0, s, partner, weight=COVER_1)
     partner = from_partner(s, "wide", 2)
     sent, s = lax.optimization_barrier((sent, s))
     far_side = swapped(sent, far)
-    near = near_own(near_index, sent, rows, s)
+    near, e = near_own(near_index, sent, rows, jnp.swapaxes(expand_basis, 1, 2), s)
     partner, near = lax.optimization_barrier((partner, near))
     s = level_step(t, 1, s, partner)
     both, high_bit = with_partner(s, "pair", 0)
     s = level_step(t, 2, s, both, high_bit)
     partner = from_partner(s, "pair", 1)
 
-    def add(name, weight, near, *sides):
-        tests = [met(keep) for keep, _ in sides]
-        sources = [side for _, side in sides]
-        return near_sides(name, weight, near_index, place, rows, tests, sources, near)
-
-    near = add(
-        "near_inner", COVER_INNER, near, (odd, in_hbm(odd_side)), (even, in_hbm(even_side))
-    )
-    near = add("near_outer", COVER_OUTER, near, (outer, outer_side))
-    near = add("near_far", COVER_FAR, near, (far, far_side))
+    for name, weight, keep, side in (
+        ("near_odd", COVER_ODD, odd, in_hbm(odd_side)),
+        ("near_even", COVER_EVEN, even, in_hbm(even_side)),
+        ("near_outer", COVER_OUTER, outer, in_hbm(outer_side)),
+        ("near_far", COVER_FAR, far, far_side),
+    ):
+        near = near_side(name, weight, near_index, place, rows, met(keep), side, near)
     return final_step(t, s, partner, e, near)
 
 

time: 58.1 us -> 56.1 us (0.966)
  blocking collectives: 12.9 us -> 11.9 us
  local copies, waits for them, and re-layouts: 1.01 us -> 0.02 us
  Pallas kernels: 14.5 us -> 13.9 us
    unnamed x8, local copies, waits for them, and re-layouts: 1.01 us -> 0.02 us
    all_gather x2, blocking collectives: 12.9 us -> 11.9 us  [with_partner(): both = lax.all_gather(block, axis, axis_index_groups=pairs)]
    ppermute x4, waiting for transfers between devices: 3.01 us -> 3.88 us  [swapped(): return lax.ppermute(block, axes, up + [(b, a) for a, b in up])]
    pallas_call x6 -> x7, Pallas kernels: 11.5 us -> 10.8 us  [the longest x4 5.94 us: near_side(): pl.pallas_call(functools.partial(side_kernel, test), out_shape=jax.ShapeD...]
  transfers between devices with their start and end apart: 7 -> 7, of which waited for: 3 -> 2; matrix products, arithmetic and copies ran while one was open for 0% -> 0% of each run, Pallas kernels for 18% -> 19%
where the time goes in v4:
time: 56.1 us; the launch traced here: 55.6 us
  starting transfers between devices  23.4 us (42%)
  Pallas kernels  13.9 us (25%)
  blocking collectives  11.9 us (21%)
  waiting for transfers between devices  5.93 us (11%)
    ppermute x4, starting transfers between devices, swapped(): return lax.ppermute(block, axes, up + [(b, a) for a, b in up])  16.3 us
    all_gather x2, blocking collectives, with_partner(): both = lax.all_gather(block, axis, axis_index_groups=pairs)  11.9 us
    ppermute x3, starting transfers between devices, from_partner(): return lax.ppermute(block, axis, [(i, i ^ 1 << bit) for i in range(count)])  7.06 us
    pallas_call x4, Pallas kernels, near_side(): pl.pallas_call(functools.partial(side_kernel, test), out_shape=jax.ShapeD...  5.94 us
    ppermute x4, waiting for transfers between devices, swapped(): return lax.ppermute(block, axes, up + [(b, a) for a, b in up])  3.88 us
    pallas_call x1, Pallas kernels, near_own(): pl.pallas_call(own_kernel, out_shape=(jax.ShapeDtypeStruct((ROWS, COLS),...  3.11 us
    pallas_call x1, Pallas kernels, project(): pl.pallas_call(project_kernel, out_shape=(jax.ShapeDtypeStruct((RANK, COL...  2.1 us
    ppermute x3, waiting for transfers between devices, from_partner(): return lax.ppermute(block, axis, [(i, i ^ 1 << bit) for i in range(count)])  2.04 us
  transfers between devices with their start and end apart: 7, of which 2 were waited for; matrix products, arithmetic and copies ran while one was open for 0% of the time, Pallas kernels for 19%

profile of v4, /device:TPU:1, one launch (start us, length us, event | category | flops | bytes accessed | tf_op | source)
XLA Modules:
  0.0 55.6 jit_solution(13987921187652862761)
XLA Ops:
  0.0 2.1 %project.1 = (bf16[192,512]{1,0:T(8,128)(2,1)S(1)}, bf16[1040,512]{1,0:T(8,128)(2,1)S(1)}, bf16[16,512]{1,0:T(8,128)(2,1)S(1)}, bf16[1,2,192,192]{3,2,1,0:T(8,128)(2,1)S(1)}) custom-call(bf16[1024,512]{1,0:T(8,128)(2,1)} %x_ref.1, bf16[2,192,512]{2,1,0:T(8,128)(2,1)} %bitcast.14, bf16[2,2,512]{2,1,0:T(2,128)(2,1)} %points_ref.1, ...), custom_call_target="tpu_custom_call" | custom-call | tf_op jit(solution)/shard_map/project/pallas_call | solution.py:106
  2.1 4.8 %collective-permute-start.6 = (bf16[1040,512]{1,0:T(8,128)(2,1)S(1)}, bf16[1040,512]{1,0:T(8,128)(2,1)}, u32[]{:S(2)}, u32[]{:S(2)}) collective-permute-start(bf16[1040,512]{1,0:T(8,128)(2,1)S(1)} %get-tuple-element.23.own_ref), channel_id=1, source_target_pairs={{0,1},{2,3},{4,5},{6,7},{8,9},{10,11},{12,13},{14,15},{16,17},{18,... | collective-permute-start | bytes 3194888 | tf_op jit(solution)/shard_map/ppermute | solution.py:340
  6.9 5.7 %all-gather = bf16[384,512]{1,0:T(8,128)(2,1)S(1)} all-gather(bf16[192,512]{1,0:T(8,128)(2,1)S(1)} %get-tuple-element.19.own_ref), channel_id=2, replica_groups={{0,16},{32,48},{64,80},{96,112},{128,144},{160,176},{192,208},{224,240}..., dimensions={0}, use_global_device_ids=true | all-gather | bytes 589824 | tf_op jit(solution)/shard_map/all_gather | solution.py:315
  12.6 0.2 level_0.2.after_ref.own_ref
  12.9 1.9 %collective-permute-start = (bf16[192,512]{1,0:T(8,128)(2,1)S(1)}, bf16[192,512]{1,0:T(8,128)(2,1)S(1)}, u32[]{:S(2)}, u32[]{:S(2)}) collective-permute-start(bf16[192,512]{1,0:T(8,128)(2,1)S(1)} %level_0.2.after_ref.own_ref), channel_id=1, source_target_pairs={{0,32},{16,48},{32,0},{48,16},{64,96},{80,112},{96,64},{112,80},{1... | collective-permute-start | bytes 589832 | tf_op jit(solution)/shard_map/ppermute | solution.py:309
  14.8 1.6 %collective-permute-start.5 = (bf16[1040,512]{1,0:T(8,128)(2,1)S(1)}, bf16[1040,512]{1,0:T(8,128)(2,1)}, u32[]{:S(2)}, u32[]{:S(2)}) collective-permute-start(bf16[1040,512]{1,0:T(8,128)(2,1)S(1)} %get-tuple-element.23.own_ref), channel_id=1, source_target_pairs={{1,2},{3,4},{5,6},{9,10},{11,12},{13,14},{17,18},{19,20},{21,22},{... | collective-permute-start | bytes 3194888 | tf_op jit(solution)/shard_map/ppermute | solution.py:340
  16.5 9.1 %collective-permute-start.4 = (bf16[1040,512]{1,0:T(8,128)(2,1)S(1)}, bf16[1040,512]{1,0:T(8,128)(2,1)}, u32[]{:S(2)}, u32[]{:S(2)}) collective-permute-start(bf16[1040,512]{1,0:T(8,128)(2,1)S(1)} %get-tuple-element.23.own_ref), channel_id=1, source_target_pairs={{7,8},{15,16},{23,24},{31,32},{39,40},{47,48},{55,56},{71,72},{79,... | collective-permute-start | bytes 3194888 | tf_op jit(solution)/shard_map/ppermute | solution.py:340
  25.6 0.3 prepare.1.t_ref
  26.0 0.0 copy-start.1
  26.0 0.3 level_0.3.after_ref.own_ref
  26.3 3.2 %collective-permute-start.1 = (bf16[192,512]{1,0:T(8,128)(2,1)S(1)}, bf16[192,512]{1,0:T(8,128)(2,1)S(1)}, u32[]{:S(2)}, u32[]{:S(2)}) collective-permute-start(bf16[192,512]{1,0:T(8,128)(2,1)S(1)} %level_0.3.after_ref.own_ref), channel_id=1, source_target_pairs={{0,64},{16,80},{32,96},{48,112},{64,0},{80,16},{96,32},{112,48},{1... | collective-permute-start | bytes 589832 | tf_op jit(solution)/shard_map/ppermute | solution.py:309
  29.5 0.7 %collective-permute-start.3 = (bf16[1040,512]{1,0:T(8,128)(2,1)S(1)}, bf16[1040,512]{1,0:T(8,128)(2,1)S(1)}, u32[]{:S(2)}, u32[]{:S(2)}) collective-permute-start(bf16[1040,512]{1,0:T(8,128)(2,1)S(1)} %get-tuple-element.23.own_ref), channel_id=1, source_target_pairs={{63,64},{127,128},{191,192},{255,256},{319,320},{383,384},{447,448... | collective-permute-start | bytes 3194888 | tf_op jit(solution)/shard_map/ppermute | solution.py:340
  30.2 3.1 %near_own.1 = (f32[1024,512]{1,0:T(8,128)S(1)}, bf16[1024,192]{1,0:T(8,128)(2,1)S(1)}) custom-call(s32[2,3]{1,0:T(2,128)S(1)} %copy-done.3, bf16[1040,512]{1,0:T(8,128)(2,1)S(1)} %get-tuple-element.23.own_ref, bf16[16,512]{1,0:T(8,128)(2,1)S(1)} %get-tuple-element.24.rows_ref, bf16[2,192,512]{2,1,0:T(8,128)(2,1)S(1)} %bitcast.13, ...), custom_call_target="tpu_custom_call" | custom-call | tf_op jit(solution)/shard_map/near_own/pallas_call | solution.py:218
  33.4 0.2 level_1.1.own_ref
  33.6 6.2 %all-gather.1 = bf16[384,512]{1,0:T(8,128)(2,1)S(1)} all-gather(bf16[192,512]{1,0:T(8,128)(2,1)S(1)} %level_1.1.own_ref), channel_id=3, replica_groups={{0,1},{2,3},{4,5},{6,7},{8,9},{10,11},{12,13},{14,15},{16,17},{18,19},{..., dimensions={0}, use_global_device_ids=true | all-gather | bytes 589824 | tf_op jit(solution)/shard_map/all_gather | solution.py:315
  39.9 0.2 level_2.1.own_ref
  40.1 1.9 %collective-permute-start.2 = (bf16[192,512]{1,0:T(8,128)(2,1)S(1)}, bf16[192,512]{1,0:T(8,128)(2,1)S(1)}, u32[]{:S(2)}, u32[]{:S(2)}) collective-permute-start(bf16[192,512]{1,0:T(8,128)(2,1)S(1)} %level_2.1.own_ref), channel_id=1, source_target_pairs={{0,2},{1,3},{2,0},{3,1},{4,6},{5,7},{6,4},{7,5},{8,10},{9,11},{10,... | collective-permute-start | bytes 589832 | tf_op jit(solution)/shard_map/ppermute | solution.py:309
  42.1 2.4 %near_odd.1._ = f32[1024,512]{1,0:T(8,128)S(1)} custom-call(s32[2,3]{1,0:T(2,128)S(1)} %copy-done.3, s32[1]{0:T(128)} %bitcast.7.wide_ref, s32[1]{0:T(128)} %bitcast.8.pair_ref, bf16[16,512]{1,0:T(8,128)(2,1)S(1)} %get-tuple-element.24.rows_ref, bf16[1040,512]{1,0:T(8,128)(2,1)} %collective-permute-done.6.source_ref, ...), custom_call_target="tpu_custom_call", output_to_operand_aliasing={{}: (5, {})} | custom-call | flops 3500000000 | bytes 4194304 | tf_op jit(solution)/shard_map/near_odd/pallas_call | solution.py:262
  44.4 0.6 %near_even.1._ = f32[1024,512]{1,0:T(8,128)S(1)} custom-call(s32[2,3]{1,0:T(2,128)S(1)} %copy-done.3, s32[1]{0:T(128)} %bitcast.7.wide_ref, s32[1]{0:T(128)} %bitcast.8.pair_ref, bf16[16,512]{1,0:T(8,128)(2,1)S(1)} %get-tuple-element.24.rows_ref, bf16[1040,512]{1,0:T(8,128)(2,1)} %collective-permute-done.5.source_ref, ...), custom_call_target="tpu_custom_call", output_to_operand_aliasing={{}: (5, {})} | custom-call | flops 1000000000 | bytes 4194304 | tf_op jit(solution)/shard_map/near_even/pallas_call | solution.py:262
  45.0 3.9 %collective-permute-done.4.source_ref = bf16[1040,512]{1,0:T(8,128)(2,1)} collective-permute-done((bf16[1040,512]{1,0:T(8,128)(2,1)S(1)}, bf16[1040,512]{1,0:T(8,128)(2,1)}, u32[]{:S(2)}, u32[]{:S(2)}) %collective-permute-start.4) | collective-permute-done | bytes 1064992 | tf_op jit(solution)/shard_map/ppermute | solution.py:340
  48.9 2.4 %near_outer.1._ = f32[1024,512]{1,0:T(8,128)S(1)} custom-call(s32[2,3]{1,0:T(2,128)S(1)} %copy-done.3, s32[1]{0:T(128)} %bitcast.7.wide_ref, s32[1]{0:T(128)} %bitcast.8.pair_ref, bf16[16,512]{1,0:T(8,128)(2,1)S(1)} %get-tuple-element.24.rows_ref, bf16[1040,512]{1,0:T(8,128)(2,1)} %collective-permute-done.4.source_ref, ...), custom_call_target="tpu_custom_call", output_to_operand_aliasing={{}: (5, {})} | custom-call | flops 6000000000 | bytes 4194304 | tf_op jit(solution)/shard_map/near_outer/pallas_call | solution.py:262
  51.3 0.6 %near_far.1.near_ref = f32[1024,512]{1,0:T(8,128)S(1)} custom-call(s32[2,3]{1,0:T(2,128)S(1)} %copy-done.3, s32[1]{0:T(128)} %bitcast.7.wide_ref, s32[1]{0:T(128)} %bitcast.8.pair_ref, bf16[16,512]{1,0:T(8,128)(2,1)S(1)} %get-tuple-element.24.rows_ref, bf16[1040,512]{1,0:T(8,128)(2,1)S(1)} %collective-permute-done.3.source_ref, ...), custom_call_target="tpu_custom_call", output_to_operand_aliasing={{}: (5, {})} | custom-call | flops 4000000000 | bytes 4194304 | tf_op jit(solution)/shard_map/near_far/pallas_call | solution.py:262
  51.9 2.0 %collective-permute-done.2.other_ref = bf16[192,512]{1,0:T(8,128)(2,1)S(1)} collective-permute-done((bf16[192,512]{1,0:T(8,128)(2,1)S(1)}, bf16[192,512]{1,0:T(8,128)(2,1)S(1)}, u32[]{:S(2)}, u32[]{:S(2)}) %collective-permute-start.2) | collective-permute-done | bytes 196640 | tf_op jit(solution)/shard_map/ppermute | solution.py:309
  54.0 1.4 %final.1 = bf16[1024,512]{1,0:T(8,128)(2,1)} custom-call(bf16[4,2,192,192]{3,2,1,0:T(8,128)(2,1)S(1)} %prepare.1.t_ref, bf16[192,512]{1,0:T(8,128)(2,1)S(1)} %level_2.1.own_ref, bf16[192,512]{1,0:T(8,128)(2,1)S(1)} %collective-permute-done.2.other_ref, bf16[1024,192]{1,0:T(8,128)(2,1)S(1)} %get-tuple-element.27.e_ref, f32[1024,512]{1,0:T(8,128)S(1)} %near_far.1.near_ref), custom_call_target="tpu_custom_call" | custom-call | tf_op jit(solution)/shard_map/final/pallas_call | solution.py:293
  (12 shorter events, 0.0 us)
Async XLA Ops:
  0.0 25.6 %copy-start = (bf16[1,5,2,192,192]{4,3,2,1,0:T(8,128)(2,1)S(1)}, bf16[1,5,2,192,192]{4,3,2,1,0:T(8,128)(2,1)}, u32[]{:S(2)}) copy-start(bf16[1,5,2,192,192]{4,3,2,1,0:T(8,128)(2,1)} %param.12) | copy-start | bytes 2211844
  0.0 25.6 %copy-start.2 = (s32[5,192]{1,0:T(8,128)S(1)}, s32[5,192]{1,0:T(8,128)}, u32[]{:S(2)}) copy-start(s32[5,192]{1,0:T(8,128)} %perm_ref.1) | copy-start | bytes 11524
  2.1 39.9 %collective-permute-start.6 = (bf16[1040,512]{1,0:T(8,128)(2,1)S(1)}, bf16[1040,512]{1,0:T(8,128)(2,1)}, u32[]{:S(2)}, u32[]{:S(2)}) collective-permute-start(bf16[1040,512]{1,0:T(8,128)(2,1)S(1)} %get-tuple-element.23.own_ref), channel_id=1, source_target_pairs={{0,1},{2,3},{4,5},{6,7},{8,9},{10,11},{12,13},{14,15},{16,17},{18,... | collective-permute-start | bytes 3194888 | tf_op jit(solution)/shard_map/ppermute | solution.py:340
  12.9 13.1 %collective-permute-start = (bf16[192,512]{1,0:T(8,128)(2,1)S(1)}, bf16[192,512]{1,0:T(8,128)(2,1)S(1)}, u32[]{:S(2)}, u32[]{:S(2)}) collective-permute-start(bf16[192,512]{1,0:T(8,128)(2,1)S(1)} %level_0.2.after_ref.own_ref), channel_id=1, source_target_pairs={{0,32},{16,48},{32,0},{48,16},{64,96},{80,112},{96,64},{112,80},{1... | collective-permute-start | bytes 589832 | tf_op jit(solution)/shard_map/ppermute | solution.py:309
  14.8 29.6 %collective-permute-start.5 = (bf16[1040,512]{1,0:T(8,128)(2,1)S(1)}, bf16[1040,512]{1,0:T(8,128)(2,1)}, u32[]{:S(2)}, u32[]{:S(2)}) collective-permute-start(bf16[1040,512]{1,0:T(8,128)(2,1)S(1)} %get-tuple-element.23.own_ref), channel_id=1, source_target_pairs={{1,2},{3,4},{5,6},{9,10},{11,12},{13,14},{17,18},{19,20},{21,22},{... | collective-permute-start | bytes 3194888 | tf_op jit(solution)/shard_map/ppermute | solution.py:340
  16.5 32.5 %collective-permute-start.4 = (bf16[1040,512]{1,0:T(8,128)(2,1)S(1)}, bf16[1040,512]{1,0:T(8,128)(2,1)}, u32[]{:S(2)}, u32[]{:S(2)}) collective-permute-start(bf16[1040,512]{1,0:T(8,128)(2,1)S(1)} %get-tuple-element.23.own_ref), channel_id=1, source_target_pairs={{7,8},{15,16},{23,24},{31,32},{39,40},{47,48},{55,56},{71,72},{79,... | collective-permute-start | bytes 3194888 | tf_op jit(solution)/shard_map/ppermute | solution.py:340
  26.0 4.3 %copy-start.1 = (bf16[2,512,192]{1,2,0:T(8,128)(2,1)S(1)}, bf16[2,512,192]{1,2,0:T(8,128)(2,1)}, u32[]{:S(2)}) copy-start(bf16[2,512,192]{1,2,0:T(8,128)(2,1)} %param.11) | copy-start | bytes 1179652
  26.0 4.3 %copy-start.3 = (s32[2,3]{1,0:T(2,128)S(1)}, s32[2,3]{1,0:T(2,128)}, u32[]{:S(2)}) copy-start(s32[2,3]{1,0:T(2,128)} %index_ref.9) | copy-start | bytes 76
  26.3 7.1 %collective-permute-start.1 = (bf16[192,512]{1,0:T(8,128)(2,1)S(1)}, bf16[192,512]{1,0:T(8,128)(2,1)S(1)}, u32[]{:S(2)}, u32[]{:S(2)}) collective-permute-start(bf16[192,512]{1,0:T(8,128)(2,1)S(1)} %level_0.3.after_ref.own_ref), channel_id=1, source_target_pairs={{0,64},{16,80},{32,96},{48,112},{64,0},{80,16},{96,32},{112,48},{1... | collective-permute-start | bytes 589832 | tf_op jit(solution)/shard_map/ppermute | solution.py:309
  29.5 21.8 %collective-permute-start.3 = (bf16[1040,512]{1,0:T(8,128)(2,1)S(1)}, bf16[1040,512]{1,0:T(8,128)(2,1)S(1)}, u32[]{:S(2)}, u32[]{:S(2)}) collective-permute-start(bf16[1040,512]{1,0:T(8,128)(2,1)S(1)} %get-tuple-element.23.own_ref), channel_id=1, source_target_pairs={{63,64},{127,128},{191,192},{255,256},{319,320},{383,384},{447,448... | collective-permute-start | bytes 3194888 | tf_op jit(solution)/shard_map/ppermute | solution.py:340
  40.1 13.8 %collective-permute-start.2 = (bf16[192,512]{1,0:T(8,128)(2,1)S(1)}, bf16[192,512]{1,0:T(8,128)(2,1)S(1)}, u32[]{:S(2)}, u32[]{:S(2)}) collective-permute-start(bf16[192,512]{1,0:T(8,128)(2,1)S(1)} %level_2.1.own_ref), channel_id=1, source_target_pairs={{0,2},{1,3},{2,0},{3,1},{4,6},{5,7},{6,4},{7,5},{8,10},{9,11},{10,... | collective-permute-start | bytes 589832 | tf_op jit(solution)/shard_map/ppermute | solution.py:309

commit v5 on v4

--- a/solution.py
+++ b/solution.py
@@ -125,15 +125,14 @@
 
 
 def prepare_kernel(transfer_ref, perm_ref, after_ref, t_ref):
-    for level in range(1, LEVELS):
-        t_ref[level - 1, 0] = transfer_ref[level, 0]
-        t_ref[level - 1, 1] = folded(transfer_ref[level, 1], perm_ref[level : level + 1, :])
+    t_ref[0, 0] = transfer_ref[1, 0]
+    t_ref[0, 1] = folded(transfer_ref[1, 1], perm_ref[1:2, :])
 
 
 def prepare(transfer, perm, after):
     return pl.pallas_call(
         prepare_kernel,
-        out_shape=jax.ShapeDtypeStruct((LEVELS - 1, 2, RANK, RANK), BF16),
+        out_shape=jax.ShapeDtypeStruct((1, 2, RANK, RANK), BF16),
         in_specs=[VMEM, VMEM, VMEM],
         out_specs=VMEM,
         compiler_params=params(),
@@ -181,29 +180,37 @@
     return rows.astype(F32) * (1.0 / FACTOR)
 
 
-def add_tile(index_ref, near_ref, target, offset, source, leaf, columns, rows):
-    used = (
+def wanted(index_ref, target, offset):
+    return (
         (index_ref[target, 0] == offset)
         | (index_ref[target, 1] == offset)
         | (index_ref[target, 2] == offset)
     )
 
-    @pl.when(used)
+
+def tile_of(columns, rows, target, leaf):
+    dx = columns[:, 2 * target : 2 * target + 1] - rows[2 * leaf : 2 * leaf + 1, :]
+    dy = columns[:, 2 * target + 1 : 2 * target + 2] - rows[2 * leaf + 1 : 2 * leaf + 2, :]
+    return lax.rsqrt(dx * dx + dy * dy + SOFT / FACTOR**2).astype(BF16)
+
+
+def add_tile(index_ref, near_ref, target, offset, source, leaf, columns, rows):
+    @pl.when(wanted(index_ref, target, offset))
     def _():
-        sx = rows[2 * leaf : 2 * leaf + 1, :]
-        sy = rows[2 * leaf + 1 : 2 * leaf + 2, :]
         held = source[leaf * LEAF : (leaf + 1) * LEAF, :]
         for start in range(0, LEAF, PIECE):
-            part = columns[start : start + PIECE]
-            dx = part[:, 2 * target : 2 * target + 1] - sx
-            dy = part[:, 2 * target + 1 : 2 * target + 2] - sy
-            tile = lax.rsqrt(dx * dx + dy * dy + SOFT / FACTOR**2).astype(BF16)
+            tile = tile_of(columns[start : start + PIECE], rows, target, leaf)
             near_ref[pl.ds(target * LEAF + start, PIECE), :] += jnp.dot(
                 tile, held, preferred_element_type=F32
             )
 
 
-def own_kernel(index_ref, own_ref, rows_ref, expand_ref, after_ref, near_ref, e_ref):
+def own_kernel(
+    index_ref, own_ref, rows_ref, expand_ref, transfer_ref, perm_ref, _, near_ref, e_ref, t_ref
+):
+    for level in range(2, LEVELS):
+        t_ref[level - 2, 0] = transfer_ref[level, 0]
+        t_ref[level - 2, 1] = folded(transfer_ref[level, 1], perm_ref[level : level + 1, :])
     for leaf in range(2):
         e_ref[leaf * LEAF : (leaf + 1) * LEAF, :] = expand_ref[leaf].T
     near_ref[...] = jnp.zeros((ROWS, COLS), F32)
@@ -214,32 +221,35 @@
             add_tile(index_ref, near_ref, target, leaf - target, own_ref, leaf, columns, rows)
 
 
-def near_own(index, own, rows, expand_t, after):
+def near_own(index, own, rows, expand_t, transfer, perm, after):
     return pl.pallas_call(
         own_kernel,
         out_shape=(
             jax.ShapeDtypeStruct((ROWS, COLS), F32),
             jax.ShapeDtypeStruct((ROWS, RANK), BF16),
+            jax.ShapeDtypeStruct((LEVELS - 2, 2, RANK, RANK), BF16),
         ),
-        in_specs=[SMEM] + [VMEM] * 4,
-        out_specs=(VMEM, VMEM),
+        in_specs=[SMEM] + [VMEM] * 6,
+        out_specs=(VMEM,) * 3,
         compiler_params=params(),
         name="near_own",
-    )(index, own, rows, expand_t, after)
+    )(index, own, rows, expand_t, transfer, perm, after)
 
 
 def side_kernel(
-    test, index_ref, wide_ref, pair_ref, rows_ref, source_ref, _, near_ref, buf, sems
+    test, table_ref, rows_ref, source_ref, _, near_ref, buf, tiles, index_ref, sems
 ):
-    low, high = test(wide_ref[0], pair_ref[0])
+    low, high = test(lax.axis_index("wide"), lax.axis_index("pair"))
     spans = ((ROWS, PACK - ROWS), (0, LEAF), (LEAF, LEAF))
     copies = []
     for i, (start, size) in enumerate(spans):
         block = pl.ds(start, size)
         copies.append(pltpu.make_async_copy(source_ref.at[block], buf.at[block], sems.at[i]))
+    table = pltpu.make_async_copy(table_ref, index_ref, sems.at[3])
 
     @pl.when(low | high)
     def _():
+        table.start()
         for copy in copies:
             copy.start()
 
@@ -247,36 +257,62 @@
 
         @pl.when(present)
         def _(shift=shift):
+            pairs = [
+                (leaf, target, shift + leaf - target)
+                for leaf in range(2)
+                for target in range(2)
+                if abs(shift + leaf - target) <= 2
+            ]
+            table.wait()
             copies[0].wait()
             columns = scaled(rows_ref[:8, :]).T
             rows = scaled(buf[ROWS : ROWS + 8, :])
-            for leaf in range(2):
-                copies[1 + leaf].wait()
-                for target in range(2):
-                    offset = shift + leaf - target
-                    if abs(offset) <= 2:
-                        add_tile(index_ref, near_ref, target, offset, buf, leaf, columns, rows)
-
-
-def near_side(name, weight, index, place, rows, test, source, near):
+            for i, (leaf, target, offset) in enumerate(pairs):
+
+                @pl.when(wanted(index_ref, target, offset))
+                def _(i=i, leaf=leaf, target=target):
+                    for start in range(0, LEAF, PIECE):
+                        tiles[i, start : start + PIECE, :] = tile_of(
+                            columns[start : start + PIECE], rows, target, leaf
+                        )
+
+            for copy in copies[1:]:
+                copy.wait()
+            for i, (leaf, target, offset) in enumerate(pairs):
+
+                @pl.when(wanted(index_ref, target, offset))
+                def _(i=i, leaf=leaf, target=target):
+                    near_ref[target * LEAF : (target + 1) * LEAF, :] += jnp.dot(
+                        tiles[i],
+                        buf[leaf * LEAF : (leaf + 1) * LEAF, :],
+                        preferred_element_type=F32,
+                    )
+
+
+def near_side(name, weight, index, rows, test, source, near):
     return pl.pallas_call(
         functools.partial(side_kernel, test),
         out_shape=jax.ShapeDtypeStruct((ROWS, COLS), F32),
-        in_specs=[SMEM] * 3 + [VMEM, ANY, VMEM],
+        in_specs=[HBM, VMEM, ANY, VMEM],
         out_specs=VMEM,
-        scratch_shapes=[pltpu.VMEM((PACK, COLS), BF16), pltpu.SemaphoreType.DMA((3,))],
-        input_output_aliases={5: 0},
+        scratch_shapes=[
+            pltpu.VMEM((PACK, COLS), BF16),
+            pltpu.VMEM((3, LEAF, LEAF), BF16),
+            pltpu.SMEM((2, 3), jnp.int32),
+            pltpu.SemaphoreType.DMA((4,)),
+        ],
+        input_output_aliases={3: 0},
         compiler_params=params(),
         cost_estimate=pl.CostEstimate(
             flops=weight, transcendentals=0, bytes_accessed=ROWS * COLS * 8
         ),
         name=name,
-    )(index, *place, rows, source, near)
+    )(in_hbm(index), rows, source, near)
 
 
 def final_kernel(t_ref, own_ref, other_ref, e_ref, near_ref, out_ref, out_buf, sems):
-    total = jnp.dot(t_ref[LEVELS - 2, 0], own_ref[...], preferred_element_type=F32)
-    total = total + jnp.dot(t_ref[LEVELS - 2, 1], other_ref[...], preferred_element_type=F32)
+    total = jnp.dot(t_ref[LEVELS - 3, 0], own_ref[...], preferred_element_type=F32)
+    total = total + jnp.dot(t_ref[LEVELS - 3, 1], other_ref[...], preferred_element_type=F32)
     s = total.astype(BF16)
     copies = []
     for i in range(ROWS // CHUNK):
@@ -346,7 +382,6 @@
 
         return test
 
-    place = (lax.axis_index("wide").reshape(1), lax.axis_index("pair").reshape(1))
     s, pack, rows, t0 = project(
         rhs, jnp.swapaxes(project_basis, 1, 2), coords, transfer[0], level_perm
     )
@@ -357,16 +392,18 @@
     sent, s = lax.optimization_barrier((pack, s))
     outer_side = swapped(sent, outer)
     even_side = swapped(sent, even)
-    t = prepare(transfer[0], level_perm, s)
-    s = level_step(t, 0, s, partner, weight=COVER_1)
+    t1 = prepare(transfer[0], level_perm, s)
+    s = level_step(t1, 0, s, partner, weight=COVER_1)
     partner = from_partner(s, "wide", 2)
     sent, s = lax.optimization_barrier((sent, s))
     far_side = swapped(sent, far)
-    near, e = near_own(near_index, sent, rows, jnp.swapaxes(expand_basis, 1, 2), s)
+    near, e, t = near_own(
+        near_index, sent, rows, jnp.swapaxes(expand_basis, 1, 2), transfer[0], level_perm, s
+    )
     partner, near = lax.optimization_barrier((partner, near))
-    s = level_step(t, 1, s, partner)
+    s = level_step(t, 0, s, partner)
     both, high_bit = with_partner(s, "pair", 0)
-    s = level_step(t, 2, s, both, high_bit)
+    s = level_step(t, 1, s, both, high_bit)
     partner = from_partner(s, "pair", 1)
 
     for name, weight, keep, side in (
@@ -375,7 +412,7 @@
         ("near_outer", COVER_OUTER, outer, in_hbm(outer_side)),
         ("near_far", COVER_FAR, far, far_side),
     ):
-        near = near_side(name, weight, near_index, place, rows, met(keep), side, near)
+        near = near_side(name, weight, near_index, rows, met(keep), side, near)
     return final_step(t, s, partner, e, near)
 
 

time: 56.1 us -> 55.9 us (level)
  Pallas kernels: 13.9 us -> 12.1 us
  waiting for transfers between devices: 5.93 us -> 6.63 us
  blocking collectives: 11.9 us -> 12.5 us
    pallas_call x1, Pallas kernels: 3.11 us -> 2.1 us  [near_own(): pl.pallas_call(own_kernel, out_shape=(jax.ShapeDtypeStruct((ROWS, COLS),...]
    pallas_call x4, Pallas kernels: 5.94 us -> 5.25 us  [near_side(): pl.pallas_call(functools.partial(side_kernel, test), out_shape=jax.ShapeD...]
  transfers between devices with their start and end apart: 7 -> 7, of which waited for: 2 -> 3; matrix products, arithmetic and copies ran while one was open for 0% -> 0% of each run, Pallas kernels for 19% -> 16%
where the time goes in v5:
time: 55.9 us; the launch traced here: 55 us
  starting transfers between devices  23.4 us (42%)
  blocking collectives  12.5 us (22%)
  Pallas kernels  12.1 us (22%)
  waiting for transfers between devices  6.63 us (12%)
    ppermute x4, starting transfers between devices, swapped(): return lax.ppermute(block, axes, up + [(b, a) for a, b in up])  16.4 us
    all_gather x2, blocking collectives, with_partner(): both = lax.all_gather(block, axis, axis_index_groups=pairs)  12.5 us
    ppermute x3, starting transfers between devices, from_partner(): return lax.ppermute(block, axis, [(i, i ^ 1 << bit) for i in range(count)])  7.06 us
    pallas_call x4, Pallas kernels, near_side(): pl.pallas_call(functools.partial(side_kernel, test), out_shape=jax.ShapeD...  5.25 us
    ppermute x4, waiting for transfers between devices, swapped(): return lax.ppermute(block, axes, up + [(b, a) for a, b in up])  4.32 us
    ppermute x3, waiting for transfers between devices, from_partner(): return lax.ppermute(block, axis, [(i, i ^ 1 << bit) for i in range(count)])  2.31 us
    pallas_call x1, Pallas kernels, near_own(): pl.pallas_call(own_kernel, out_shape=(jax.ShapeDtypeStruct((ROWS, COLS),...  2.1 us
    pallas_call x1, Pallas kernels, project(): pl.pallas_call(project_kernel, out_shape=(jax.ShapeDtypeStruct((RANK, COL...  2.1 us
  transfers between devices with their start and end apart: 7, of which 3 were waited for; matrix products, arithmetic and copies ran while one was open for 0% of the time, Pallas kernels for 16%

profile of v5, /device:TPU:1, one launch (start us, length us, event | category | flops | bytes accessed | tf_op | source)
XLA Modules:
  0.0 55.0 jit_solution(9560471249606780239)
XLA Ops:
  0.0 2.1 %project.1 = (bf16[192,512]{1,0:T(8,128)(2,1)S(1)}, bf16[1040,512]{1,0:T(8,128)(2,1)S(1)}, bf16[16,512]{1,0:T(8,128)(2,1)S(1)}, bf16[1,2,192,192]{3,2,1,0:T(8,128)(2,1)S(1)}) custom-call(bf16[1024,512]{1,0:T(8,128)(2,1)} %x_ref.1, bf16[2,192,512]{2,1,0:T(8,128)(2,1)} %bitcast.13, bf16[2,2,512]{2,1,0:T(2,128)(2,1)} %points_ref.1, ...), custom_call_target="tpu_custom_call" | custom-call | tf_op jit(solution)/shard_map/project/pallas_call | solution.py:106
  2.1 4.8 %collective-permute-start.6 = (bf16[1040,512]{1,0:T(8,128)(2,1)S(1)}, bf16[1040,512]{1,0:T(8,128)(2,1)}, u32[]{:S(2)}, u32[]{:S(2)}) collective-permute-start(bf16[1040,512]{1,0:T(8,128)(2,1)S(1)} %get-tuple-element.23.own_ref), channel_id=1, source_target_pairs={{0,1},{2,3},{4,5},{6,7},{8,9},{10,11},{12,13},{14,15},{16,17},{18,... | collective-permute-start | bytes 3194888 | tf_op jit(solution)/shard_map/ppermute | solution.py:376
  6.9 5.7 %all-gather = bf16[384,512]{1,0:T(8,128)(2,1)S(1)} all-gather(bf16[192,512]{1,0:T(8,128)(2,1)S(1)} %get-tuple-element.20.own_ref), channel_id=2, replica_groups={{0,16},{32,48},{64,80},{96,112},{128,144},{160,176},{192,208},{224,240}..., dimensions={0}, use_global_device_ids=true | all-gather | bytes 589824 | tf_op jit(solution)/shard_map/all_gather | solution.py:351
  12.6 0.2 level_0.3.after_ref.own_ref
  12.9 1.9 %collective-permute-start = (bf16[192,512]{1,0:T(8,128)(2,1)S(1)}, bf16[192,512]{1,0:T(8,128)(2,1)S(1)}, u32[]{:S(2)}, u32[]{:S(2)}) collective-permute-start(bf16[192,512]{1,0:T(8,128)(2,1)S(1)} %level_0.3.after_ref.own_ref), channel_id=1, source_target_pairs={{0,32},{16,48},{32,0},{48,16},{64,96},{80,112},{96,64},{112,80},{1... | collective-permute-start | bytes 589832 | tf_op jit(solution)/shard_map/ppermute | solution.py:345
  14.8 1.7 %collective-permute-start.5 = (bf16[1040,512]{1,0:T(8,128)(2,1)S(1)}, bf16[1040,512]{1,0:T(8,128)(2,1)}, u32[]{:S(2)}, u32[]{:S(2)}) collective-permute-start(bf16[1040,512]{1,0:T(8,128)(2,1)S(1)} %get-tuple-element.23.own_ref), channel_id=1, source_target_pairs={{1,2},{3,4},{5,6},{9,10},{11,12},{13,14},{17,18},{19,20},{21,22},{... | collective-permute-start | bytes 3194888 | tf_op jit(solution)/shard_map/ppermute | solution.py:376
  16.5 9.1 %collective-permute-start.4 = (bf16[1040,512]{1,0:T(8,128)(2,1)S(1)}, bf16[1040,512]{1,0:T(8,128)(2,1)}, u32[]{:S(2)}, u32[]{:S(2)}) collective-permute-start(bf16[1040,512]{1,0:T(8,128)(2,1)S(1)} %get-tuple-element.23.own_ref), channel_id=1, source_target_pairs={{7,8},{15,16},{23,24},{31,32},{39,40},{47,48},{55,56},{71,72},{79,... | collective-permute-start | bytes 3194888 | tf_op jit(solution)/shard_map/ppermute | solution.py:376
  25.6 0.2 prepare.1.t_ref
  25.9 0.3 level_0.4._.own_ref
  26.1 3.2 %collective-permute-start.1 = (bf16[192,512]{1,0:T(8,128)(2,1)S(1)}, bf16[192,512]{1,0:T(8,128)(2,1)S(1)}, u32[]{:S(2)}, u32[]{:S(2)}) collective-permute-start(bf16[192,512]{1,0:T(8,128)(2,1)S(1)} %level_0.4._.own_ref), channel_id=1, source_target_pairs={{0,64},{16,80},{32,96},{48,112},{64,0},{80,16},{96,32},{112,48},{1... | collective-permute-start | bytes 589832 | tf_op jit(solution)/shard_map/ppermute | solution.py:345
  29.4 0.7 %collective-permute-start.3 = (bf16[1040,512]{1,0:T(8,128)(2,1)S(1)}, bf16[1040,512]{1,0:T(8,128)(2,1)S(1)}, u32[]{:S(2)}, u32[]{:S(2)}) collective-permute-start(bf16[1040,512]{1,0:T(8,128)(2,1)S(1)} %get-tuple-element.23.own_ref), channel_id=1, source_target_pairs={{63,64},{127,128},{191,192},{255,256},{319,320},{383,384},{447,448... | collective-permute-start | bytes 3194888 | tf_op jit(solution)/shard_map/ppermute | solution.py:376
  30.1 2.1 %near_own.1 = (f32[1024,512]{1,0:T(8,128)S(1)}, bf16[1024,192]{1,0:T(8,128)(2,1)S(1)}, bf16[3,2,192,192]{3,2,1,0:T(8,128)(2,1)S(1)}) custom-call(s32[2,3]{1,0:T(2,128)S(1)} %copy-done.3, bf16[1040,512]{1,0:T(8,128)(2,1)S(1)} %get-tuple-element.23.own_ref, bf16[16,512]{1,0:T(8,128)(2,1)S(1)} %get-tuple-element.24.rows_ref, bf16[2,192,512]{2,1,0:T(8,128)(2,1)S(1)} %bitcast.12, ...), custom_call_target="tpu_custom_call" | custom-call | tf_op jit(solution)/shard_map/near_own/pallas_call | solution.py:225
  32.2 0.6 %collective-permute-done.1.other_ref = bf16[192,512]{1,0:T(8,128)(2,1)S(1)} collective-permute-done((bf16[192,512]{1,0:T(8,128)(2,1)S(1)}, bf16[192,512]{1,0:T(8,128)(2,1)S(1)}, u32[]{:S(2)}, u32[]{:S(2)}) %collective-permute-start.1) | collective-permute-done | bytes 196640 | tf_op jit(solution)/shard_map/ppermute | solution.py:345
  32.8 0.2 level_0.5.own_ref
  33.1 6.8 %all-gather.1 = bf16[384,512]{1,0:T(8,128)(2,1)S(1)} all-gather(bf16[192,512]{1,0:T(8,128)(2,1)S(1)} %level_0.5.own_ref), channel_id=3, replica_groups={{0,1},{2,3},{4,5},{6,7},{8,9},{10,11},{12,13},{14,15},{16,17},{18,19},{..., dimensions={0}, use_global_device_ids=true | all-gather | bytes 589824 | tf_op jit(solution)/shard_map/all_gather | solution.py:351
  39.9 0.2 level_1.1.own_ref
  40.1 1.9 %collective-permute-start.2 = (bf16[192,512]{1,0:T(8,128)(2,1)S(1)}, bf16[192,512]{1,0:T(8,128)(2,1)S(1)}, u32[]{:S(2)}, u32[]{:S(2)}) collective-permute-start(bf16[192,512]{1,0:T(8,128)(2,1)S(1)} %level_1.1.own_ref), channel_id=1, source_target_pairs={{0,2},{1,3},{2,0},{3,1},{4,6},{5,7},{6,4},{7,5},{8,10},{9,11},{10,... | collective-permute-start | bytes 589832 | tf_op jit(solution)/shard_map/ppermute | solution.py:345
  42.1 2.5 %near_odd.1._ = f32[1024,512]{1,0:T(8,128)S(1)} custom-call(s32[2,3]{1,0:T(2,128)} %table_ref.7, bf16[16,512]{1,0:T(8,128)(2,1)S(1)} %get-tuple-element.24.rows_ref, bf16[1040,512]{1,0:T(8,128)(2,1)} %collective-permute-done.6.source_ref, f32[1024,512]{1,0:T(8,128)S(1)} %get-tuple-element.30._), custom_call_target="tpu_custom_call", output_to_operand_aliasing={{}: (3, {})} | custom-call | flops 3500000000 | bytes 4194304 | tf_op jit(solution)/shard_map/near_odd/pallas_call | solution.py:293
  44.6 0.1 near_even.1._
  44.6 4.3 %collective-permute-done.4.source_ref = bf16[1040,512]{1,0:T(8,128)(2,1)} collective-permute-done((bf16[1040,512]{1,0:T(8,128)(2,1)S(1)}, bf16[1040,512]{1,0:T(8,128)(2,1)}, u32[]{:S(2)}, u32[]{:S(2)}) %collective-permute-start.4) | collective-permute-done | bytes 1064992 | tf_op jit(solution)/shard_map/ppermute | solution.py:376
  49.0 2.6 %near_outer.1._ = f32[1024,512]{1,0:T(8,128)S(1)} custom-call(s32[2,3]{1,0:T(2,128)} %table_ref.7, bf16[16,512]{1,0:T(8,128)(2,1)S(1)} %get-tuple-element.24.rows_ref, bf16[1040,512]{1,0:T(8,128)(2,1)} %collective-permute-done.4.source_ref, f32[1024,512]{1,0:T(8,128)S(1)} %near_even.1._), custom_call_target="tpu_custom_call", output_to_operand_aliasing={{}: (3, {})} | custom-call | flops 6000000000 | bytes 4194304 | tf_op jit(solution)/shard_map/near_outer/pallas_call | solution.py:293
  51.6 0.1 near_far.1.near_ref
  51.7 1.7 %collective-permute-done.2.other_ref = bf16[192,512]{1,0:T(8,128)(2,1)S(1)} collective-permute-done((bf16[192,512]{1,0:T(8,128)(2,1)S(1)}, bf16[192,512]{1,0:T(8,128)(2,1)S(1)}, u32[]{:S(2)}, u32[]{:S(2)}) %collective-permute-start.2) | collective-permute-done | bytes 196640 | tf_op jit(solution)/shard_map/ppermute | solution.py:345
  53.4 1.4 %final.1 = bf16[1024,512]{1,0:T(8,128)(2,1)} custom-call(bf16[3,2,192,192]{3,2,1,0:T(8,128)(2,1)S(1)} %get-tuple-element.26.t_ref, bf16[192,512]{1,0:T(8,128)(2,1)S(1)} %level_1.1.own_ref, bf16[192,512]{1,0:T(8,128)(2,1)S(1)} %collective-permute-done.2.other_ref, bf16[1024,192]{1,0:T(8,128)(2,1)S(1)} %get-tuple-element.29.e_ref, ...), custom_call_target="tpu_custom_call" | custom-call | tf_op jit(solution)/shard_map/final/pallas_call | solution.py:329
  (12 shorter events, 0.0 us)
Async XLA Ops:
  0.0 25.6 %copy-start = (bf16[1,5,2,192,192]{4,3,2,1,0:T(8,128)(2,1)S(1)}, bf16[1,5,2,192,192]{4,3,2,1,0:T(8,128)(2,1)}, u32[]{:S(2)}) copy-start(bf16[1,5,2,192,192]{4,3,2,1,0:T(8,128)(2,1)} %param.12) | copy-start | bytes 2211844
  0.0 25.6 %copy-start.2 = (s32[5,192]{1,0:T(8,128)S(1)}, s32[5,192]{1,0:T(8,128)}, u32[]{:S(2)}) copy-start(s32[5,192]{1,0:T(8,128)} %perm_ref.3) | copy-start | bytes 11524
  2.1 39.9 %collective-permute-start.6 = (bf16[1040,512]{1,0:T(8,128)(2,1)S(1)}, bf16[1040,512]{1,0:T(8,128)(2,1)}, u32[]{:S(2)}, u32[]{:S(2)}) collective-permute-start(bf16[1040,512]{1,0:T(8,128)(2,1)S(1)} %get-tuple-element.23.own_ref), channel_id=1, source_target_pairs={{0,1},{2,3},{4,5},{6,7},{8,9},{10,11},{12,13},{14,15},{16,17},{18,... | collective-permute-start | bytes 3194888 | tf_op jit(solution)/shard_map/ppermute | solution.py:376
  12.9 13.0 %collective-permute-start = (bf16[192,512]{1,0:T(8,128)(2,1)S(1)}, bf16[192,512]{1,0:T(8,128)(2,1)S(1)}, u32[]{:S(2)}, u32[]{:S(2)}) collective-permute-start(bf16[192,512]{1,0:T(8,128)(2,1)S(1)} %level_0.3.after_ref.own_ref), channel_id=1, source_target_pairs={{0,32},{16,48},{32,0},{48,16},{64,96},{80,112},{96,64},{112,80},{1... | collective-permute-start | bytes 589832 | tf_op jit(solution)/shard_map/ppermute | solution.py:345
  14.8 29.7 %collective-permute-start.5 = (bf16[1040,512]{1,0:T(8,128)(2,1)S(1)}, bf16[1040,512]{1,0:T(8,128)(2,1)}, u32[]{:S(2)}, u32[]{:S(2)}) collective-permute-start(bf16[1040,512]{1,0:T(8,128)(2,1)S(1)} %get-tuple-element.23.own_ref), channel_id=1, source_target_pairs={{1,2},{3,4},{5,6},{9,10},{11,12},{13,14},{17,18},{19,20},{21,22},{... | collective-permute-start | bytes 3194888 | tf_op jit(solution)/shard_map/ppermute | solution.py:376
  16.5 32.5 %collective-permute-start.4 = (bf16[1040,512]{1,0:T(8,128)(2,1)S(1)}, bf16[1040,512]{1,0:T(8,128)(2,1)}, u32[]{:S(2)}, u32[]{:S(2)}) collective-permute-start(bf16[1040,512]{1,0:T(8,128)(2,1)S(1)} %get-tuple-element.23.own_ref), channel_id=1, source_target_pairs={{7,8},{15,16},{23,24},{31,32},{39,40},{47,48},{55,56},{71,72},{79,... | collective-permute-start | bytes 3194888 | tf_op jit(solution)/shard_map/ppermute | solution.py:376
  25.8 4.3 %copy-start.1 = (bf16[2,512,192]{1,2,0:T(8,128)(2,1)S(1)}, bf16[2,512,192]{1,2,0:T(8,128)(2,1)}, u32[]{:S(2)}) copy-start(bf16[2,512,192]{1,2,0:T(8,128)(2,1)} %param.11) | copy-start | bytes 1179652
  25.9 4.3 %copy-start.3 = (s32[2,3]{1,0:T(2,128)S(1)}, s32[2,3]{1,0:T(2,128)}, u32[]{:S(2)}) copy-start(s32[2,3]{1,0:T(2,128)} %table_ref.7) | copy-start | bytes 76
  26.1 6.7 %collective-permute-start.1 = (bf16[192,512]{1,0:T(8,128)(2,1)S(1)}, bf16[192,512]{1,0:T(8,128)(2,1)S(1)}, u32[]{:S(2)}, u32[]{:S(2)}) collective-permute-start(bf16[192,512]{1,0:T(8,128)(2,1)S(1)} %level_0.4._.own_ref), channel_id=1, source_target_pairs={{0,64},{16,80},{32,96},{48,112},{64,0},{80,16},{96,32},{112,48},{1... | collective-permute-start | bytes 589832 | tf_op jit(solution)/shard_map/ppermute | solution.py:345
  29.4 22.2 %collective-permute-start.3 = (bf16[1040,512]{1,0:T(8,128)(2,1)S(1)}, bf16[1040,512]{1,0:T(8,128)(2,1)S(1)}, u32[]{:S(2)}, u32[]{:S(2)}) collective-permute-start(bf16[1040,512]{1,0:T(8,128)(2,1)S(1)} %get-tuple-element.23.own_ref), channel_id=1, source_target_pairs={{63,64},{127,128},{191,192},{255,256},{319,320},{383,384},{447,448... | collective-permute-start | bytes 3194888 | tf_op jit(solution)/shard_map/ppermute | solution.py:376
  40.1 13.2 %collective-permute-start.2 = (bf16[192,512]{1,0:T(8,128)(2,1)S(1)}, bf16[192,512]{1,0:T(8,128)(2,1)S(1)}, u32[]{:S(2)}, u32[]{:S(2)}) collective-permute-start(bf16[192,512]{1,0:T(8,128)(2,1)S(1)} %level_1.1.own_ref), channel_id=1, source_target_pairs={{0,2},{1,3},{2,0},{3,1},{4,6},{5,7},{6,4},{7,5},{8,10},{9,11},{10,... | collective-permute-start | bytes 589832 | tf_op jit(solution)/shard_map/ppermute | solution.py:345

commit v6 on v5

--- a/solution.py
+++ b/solution.py
@@ -17,7 +17,7 @@
 ROWS = 1024
 PACK = ROWS + 16
 RUN = 8
-CHUNK = 128
+CHUNK = 256
 PIECE = 128
 COVER_1 = 3_000_000_000
 COVER_ODD = 3_500_000_000

time: 55.9 us -> 55.9 us (level)
    ppermute x3, waiting for transfers between devices: 2.31 us -> 1.54 us  [from_partner(): return lax.ppermute(block, axis, [(i, i ^ 1 << bit) for i in range(count)])]
    ppermute x4, waiting for transfers between devices: 4.32 us -> 5.09 us  [swapped(): return lax.ppermute(block, axes, up + [(b, a) for a, b in up])]
where the time goes in v6:
time: 55.9 us; the launch traced here: 55 us
  starting transfers between devices  23.4 us (42%)
  blocking collectives  12.5 us (22%)
  Pallas kernels  12.1 us (22%)
  waiting for transfers between devices  6.63 us (12%)
    ppermute x4, starting transfers between devices, swapped(): return lax.ppermute(block, axes, up + [(b, a) for a, b in up])  16.4 us
    all_gather x2, blocking collectives, with_partner(): both = lax.all_gather(block, axis, axis_index_groups=pairs)  12.5 us
    ppermute x3, starting transfers between devices, from_partner(): return lax.ppermute(block, axis, [(i, i ^ 1 << bit) for i in range(count)])  7.06 us
    pallas_call x4, Pallas kernels, near_side(): pl.pallas_call(functools.partial(side_kernel, test), out_shape=jax.ShapeD...  5.25 us
    ppermute x4, waiting for transfers between devices, swapped(): return lax.ppermute(block, axes, up + [(b, a) for a, b in up])  5.09 us
    pallas_call x1, Pallas kernels, near_own(): pl.pallas_call(own_kernel, out_shape=(jax.ShapeDtypeStruct((ROWS, COLS),...  2.1 us
    pallas_call x1, Pallas kernels, project(): pl.pallas_call(project_kernel, out_shape=(jax.ShapeDtypeStruct((RANK, COL...  2.1 us
    ppermute x3, waiting for transfers between devices, from_partner(): return lax.ppermute(block, axis, [(i, i ^ 1 << bit) for i in range(count)])  1.54 us
  transfers between devices with their start and end apart: 7, of which 3 were waited for; matrix products, arithmetic and copies ran while one was open for 0% of the time, Pallas kernels for 16%

profile of v6, /device:TPU:1, one launch (start us, length us, event | category | flops | bytes accessed | tf_op | source)
XLA Modules:
  0.0 55.0 jit_solution(12952345712075893212)
XLA Ops:
  0.0 2.1 %project.1 = (bf16[192,512]{1,0:T(8,128)(2,1)S(1)}, bf16[1040,512]{1,0:T(8,128)(2,1)S(1)}, bf16[16,512]{1,0:T(8,128)(2,1)S(1)}, bf16[1,2,192,192]{3,2,1,0:T(8,128)(2,1)S(1)}) custom-call(bf16[1024,512]{1,0:T(8,128)(2,1)} %x_ref.1, bf16[2,192,512]{2,1,0:T(8,128)(2,1)} %bitcast.13, bf16[2,2,512]{2,1,0:T(2,128)(2,1)} %points_ref.1, ...), custom_call_target="tpu_custom_call" | custom-call | tf_op jit(solution)/shard_map/project/pallas_call | solution.py:106
  2.1 4.8 %collective-permute-start.6 = (bf16[1040,512]{1,0:T(8,128)(2,1)S(1)}, bf16[1040,512]{1,0:T(8,128)(2,1)}, u32[]{:S(2)}, u32[]{:S(2)}) collective-permute-start(bf16[1040,512]{1,0:T(8,128)(2,1)S(1)} %get-tuple-element.23.own_ref), channel_id=1, source_target_pairs={{0,1},{2,3},{4,5},{6,7},{8,9},{10,11},{12,13},{14,15},{16,17},{18,... | collective-permute-start | bytes 3194888 | tf_op jit(solution)/shard_map/ppermute | solution.py:376
  6.9 5.7 %all-gather = bf16[384,512]{1,0:T(8,128)(2,1)S(1)} all-gather(bf16[192,512]{1,0:T(8,128)(2,1)S(1)} %get-tuple-element.20.own_ref), channel_id=2, replica_groups={{0,16},{32,48},{64,80},{96,112},{128,144},{160,176},{192,208},{224,240}..., dimensions={0}, use_global_device_ids=true | all-gather | bytes 589824 | tf_op jit(solution)/shard_map/all_gather | solution.py:351
  12.6 0.2 level_0.3.after_ref.own_ref
  12.9 1.9 %collective-permute-start = (bf16[192,512]{1,0:T(8,128)(2,1)S(1)}, bf16[192,512]{1,0:T(8,128)(2,1)S(1)}, u32[]{:S(2)}, u32[]{:S(2)}) collective-permute-start(bf16[192,512]{1,0:T(8,128)(2,1)S(1)} %level_0.3.after_ref.own_ref), channel_id=1, source_target_pairs={{0,32},{16,48},{32,0},{48,16},{64,96},{80,112},{96,64},{112,80},{1... | collective-permute-start | bytes 589832 | tf_op jit(solution)/shard_map/ppermute | solution.py:345
  14.8 1.7 %collective-permute-start.5 = (bf16[1040,512]{1,0:T(8,128)(2,1)S(1)}, bf16[1040,512]{1,0:T(8,128)(2,1)}, u32[]{:S(2)}, u32[]{:S(2)}) collective-permute-start(bf16[1040,512]{1,0:T(8,128)(2,1)S(1)} %get-tuple-element.23.own_ref), channel_id=1, source_target_pairs={{1,2},{3,4},{5,6},{9,10},{11,12},{13,14},{17,18},{19,20},{21,22},{... | collective-permute-start | bytes 3194888 | tf_op jit(solution)/shard_map/ppermute | solution.py:376
  16.5 9.1 %collective-permute-start.4 = (bf16[1040,512]{1,0:T(8,128)(2,1)S(1)}, bf16[1040,512]{1,0:T(8,128)(2,1)}, u32[]{:S(2)}, u32[]{:S(2)}) collective-permute-start(bf16[1040,512]{1,0:T(8,128)(2,1)S(1)} %get-tuple-element.23.own_ref), channel_id=1, source_target_pairs={{7,8},{15,16},{23,24},{31,32},{39,40},{47,48},{55,56},{71,72},{79,... | collective-permute-start | bytes 3194888 | tf_op jit(solution)/shard_map/ppermute | solution.py:376
  25.6 0.2 prepare.1.t_ref
  25.9 0.3 level_0.4._.own_ref
  26.1 3.2 %collective-permute-start.1 = (bf16[192,512]{1,0:T(8,128)(2,1)S(1)}, bf16[192,512]{1,0:T(8,128)(2,1)S(1)}, u32[]{:S(2)}, u32[]{:S(2)}) collective-permute-start(bf16[192,512]{1,0:T(8,128)(2,1)S(1)} %level_0.4._.own_ref), channel_id=1, source_target_pairs={{0,64},{16,80},{32,96},{48,112},{64,0},{80,16},{96,32},{112,48},{1... | collective-permute-start | bytes 589832 | tf_op jit(solution)/shard_map/ppermute | solution.py:345
  29.4 0.7 %collective-permute-start.3 = (bf16[1040,512]{1,0:T(8,128)(2,1)S(1)}, bf16[1040,512]{1,0:T(8,128)(2,1)S(1)}, u32[]{:S(2)}, u32[]{:S(2)}) collective-permute-start(bf16[1040,512]{1,0:T(8,128)(2,1)S(1)} %get-tuple-element.23.own_ref), channel_id=1, source_target_pairs={{63,64},{127,128},{191,192},{255,256},{319,320},{383,384},{447,448... | collective-permute-start | bytes 3194888 | tf_op jit(solution)/shard_map/ppermute | solution.py:376
  30.1 2.1 %near_own.1 = (f32[1024,512]{1,0:T(8,128)S(1)}, bf16[1024,192]{1,0:T(8,128)(2,1)S(1)}, bf16[3,2,192,192]{3,2,1,0:T(8,128)(2,1)S(1)}) custom-call(s32[2,3]{1,0:T(2,128)S(1)} %copy-done.3, bf16[1040,512]{1,0:T(8,128)(2,1)S(1)} %get-tuple-element.23.own_ref, bf16[16,512]{1,0:T(8,128)(2,1)S(1)} %get-tuple-element.24.rows_ref, bf16[2,192,512]{2,1,0:T(8,128)(2,1)S(1)} %bitcast.12, ...), custom_call_target="tpu_custom_call" | custom-call | tf_op jit(solution)/shard_map/near_own/pallas_call | solution.py:225
  32.2 0.6 %collective-permute-done.1.other_ref = bf16[192,512]{1,0:T(8,128)(2,1)S(1)} collective-permute-done((bf16[192,512]{1,0:T(8,128)(2,1)S(1)}, bf16[192,512]{1,0:T(8,128)(2,1)S(1)}, u32[]{:S(2)}, u32[]{:S(2)}) %collective-permute-start.1) | collective-permute-done | bytes 196640 | tf_op jit(solution)/shard_map/ppermute | solution.py:345
  32.8 0.2 level_0.5.own_ref
  33.1 6.8 %all-gather.1 = bf16[384,512]{1,0:T(8,128)(2,1)S(1)} all-gather(bf16[192,512]{1,0:T(8,128)(2,1)S(1)} %level_0.5.own_ref), channel_id=3, replica_groups={{0,1},{2,3},{4,5},{6,7},{8,9},{10,11},{12,13},{14,15},{16,17},{18,19},{..., dimensions={0}, use_global_device_ids=true | all-gather | bytes 589824 | tf_op jit(solution)/shard_map/all_gather | solution.py:351
  39.9 0.2 level_1.1.own_ref
  40.1 1.9 %collective-permute-start.2 = (bf16[192,512]{1,0:T(8,128)(2,1)S(1)}, bf16[192,512]{1,0:T(8,128)(2,1)S(1)}, u32[]{:S(2)}, u32[]{:S(2)}) collective-permute-start(bf16[192,512]{1,0:T(8,128)(2,1)S(1)} %level_1.1.own_ref), channel_id=1, source_target_pairs={{0,2},{1,3},{2,0},{3,1},{4,6},{5,7},{6,4},{7,5},{8,10},{9,11},{10,... | collective-permute-start | bytes 589832 | tf_op jit(solution)/shard_map/ppermute | solution.py:345
  42.1 1.7 %near_odd.1._ = f32[1024,512]{1,0:T(8,128)S(1)} custom-call(s32[2,3]{1,0:T(2,128)} %table_ref.7, bf16[16,512]{1,0:T(8,128)(2,1)S(1)} %get-tuple-element.24.rows_ref, bf16[1040,512]{1,0:T(8,128)(2,1)} %collective-permute-done.6.source_ref, f32[1024,512]{1,0:T(8,128)S(1)} %get-tuple-element.30._), custom_call_target="tpu_custom_call", output_to_operand_aliasing={{}: (3, {})} | custom-call | flops 3500000000 | bytes 4194304 | tf_op jit(solution)/shard_map/near_odd/pallas_call | solution.py:293
  43.8 0.1 near_even.1._
  43.9 5.1 %collective-permute-done.4.source_ref = bf16[1040,512]{1,0:T(8,128)(2,1)} collective-permute-done((bf16[1040,512]{1,0:T(8,128)(2,1)S(1)}, bf16[1040,512]{1,0:T(8,128)(2,1)}, u32[]{:S(2)}, u32[]{:S(2)}) %collective-permute-start.4) | collective-permute-done | bytes 1064992 | tf_op jit(solution)/shard_map/ppermute | solution.py:376
  49.0 3.4 %near_outer.1._ = f32[1024,512]{1,0:T(8,128)S(1)} custom-call(s32[2,3]{1,0:T(2,128)} %table_ref.7, bf16[16,512]{1,0:T(8,128)(2,1)S(1)} %get-tuple-element.24.rows_ref, bf16[1040,512]{1,0:T(8,128)(2,1)} %collective-permute-done.4.source_ref, f32[1024,512]{1,0:T(8,128)S(1)} %near_even.1._), custom_call_target="tpu_custom_call", output_to_operand_aliasing={{}: (3, {})} | custom-call | flops 6000000000 | bytes 4194304 | tf_op jit(solution)/shard_map/near_outer/pallas_call | solution.py:293
  52.4 0.1 near_far.1.near_ref
  52.5 0.9 %collective-permute-done.2.other_ref = bf16[192,512]{1,0:T(8,128)(2,1)S(1)} collective-permute-done((bf16[192,512]{1,0:T(8,128)(2,1)S(1)}, bf16[192,512]{1,0:T(8,128)(2,1)S(1)}, u32[]{:S(2)}, u32[]{:S(2)}) %collective-permute-start.2) | collective-permute-done | bytes 196640 | tf_op jit(solution)/shard_map/ppermute | solution.py:345
  53.4 1.4 %final.1 = bf16[1024,512]{1,0:T(8,128)(2,1)} custom-call(bf16[3,2,192,192]{3,2,1,0:T(8,128)(2,1)S(1)} %get-tuple-element.26.t_ref, bf16[192,512]{1,0:T(8,128)(2,1)S(1)} %level_1.1.own_ref, bf16[192,512]{1,0:T(8,128)(2,1)S(1)} %collective-permute-done.2.other_ref, bf16[1024,192]{1,0:T(8,128)(2,1)S(1)} %get-tuple-element.29.e_ref, ...), custom_call_target="tpu_custom_call" | custom-call | tf_op jit(solution)/shard_map/final/pallas_call | solution.py:329
  (12 shorter events, 0.0 us)
Async XLA Ops:
  0.0 25.6 %copy-start = (bf16[1,5,2,192,192]{4,3,2,1,0:T(8,128)(2,1)S(1)}, bf16[1,5,2,192,192]{4,3,2,1,0:T(8,128)(2,1)}, u32[]{:S(2)}) copy-start(bf16[1,5,2,192,192]{4,3,2,1,0:T(8,128)(2,1)} %param.12) | copy-start | bytes 2211844
  0.0 25.6 %copy-start.2 = (s32[5,192]{1,0:T(8,128)S(1)}, s32[5,192]{1,0:T(8,128)}, u32[]{:S(2)}) copy-start(s32[5,192]{1,0:T(8,128)} %perm_ref.3) | copy-start | bytes 11524
  2.1 39.9 %collective-permute-start.6 = (bf16[1040,512]{1,0:T(8,128)(2,1)S(1)}, bf16[1040,512]{1,0:T(8,128)(2,1)}, u32[]{:S(2)}, u32[]{:S(2)}) collective-permute-start(bf16[1040,512]{1,0:T(8,128)(2,1)S(1)} %get-tuple-element.23.own_ref), channel_id=1, source_target_pairs={{0,1},{2,3},{4,5},{6,7},{8,9},{10,11},{12,13},{14,15},{16,17},{18,... | collective-permute-start | bytes 3194888 | tf_op jit(solution)/shard_map/ppermute | solution.py:376
  12.9 13.0 %collective-permute-start = (bf16[192,512]{1,0:T(8,128)(2,1)S(1)}, bf16[192,512]{1,0:T(8,128)(2,1)S(1)}, u32[]{:S(2)}, u32[]{:S(2)}) collective-permute-start(bf16[192,512]{1,0:T(8,128)(2,1)S(1)} %level_0.3.after_ref.own_ref), channel_id=1, source_target_pairs={{0,32},{16,48},{32,0},{48,16},{64,96},{80,112},{96,64},{112,80},{1... | collective-permute-start | bytes 589832 | tf_op jit(solution)/shard_map/ppermute | solution.py:345
  14.8 29.0 %collective-permute-start.5 = (bf16[1040,512]{1,0:T(8,128)(2,1)S(1)}, bf16[1040,512]{1,0:T(8,128)(2,1)}, u32[]{:S(2)}, u32[]{:S(2)}) collective-permute-start(bf16[1040,512]{1,0:T(8,128)(2,1)S(1)} %get-tuple-element.23.own_ref), channel_id=1, source_target_pairs={{1,2},{3,4},{5,6},{9,10},{11,12},{13,14},{17,18},{19,20},{21,22},{... | collective-permute-start | bytes 3194888 | tf_op jit(solution)/shard_map/ppermute | solution.py:376
  16.5 32.5 %collective-permute-start.4 = (bf16[1040,512]{1,0:T(8,128)(2,1)S(1)}, bf16[1040,512]{1,0:T(8,128)(2,1)}, u32[]{:S(2)}, u32[]{:S(2)}) collective-permute-start(bf16[1040,512]{1,0:T(8,128)(2,1)S(1)} %get-tuple-element.23.own_ref), channel_id=1, source_target_pairs={{7,8},{15,16},{23,24},{31,32},{39,40},{47,48},{55,56},{71,72},{79,... | collective-permute-start | bytes 3194888 | tf_op jit(solution)/shard_map/ppermute | solution.py:376
  25.8 4.3 %copy-start.1 = (bf16[2,512,192]{1,2,0:T(8,128)(2,1)S(1)}, bf16[2,512,192]{1,2,0:T(8,128)(2,1)}, u32[]{:S(2)}) copy-start(bf16[2,512,192]{1,2,0:T(8,128)(2,1)} %param.11) | copy-start | bytes 1179652
  25.9 4.3 %copy-start.3 = (s32[2,3]{1,0:T(2,128)S(1)}, s32[2,3]{1,0:T(2,128)}, u32[]{:S(2)}) copy-start(s32[2,3]{1,0:T(2,128)} %table_ref.7) | copy-start | bytes 76
  26.1 6.7 %collective-permute-start.1 = (bf16[192,512]{1,0:T(8,128)(2,1)S(1)}, bf16[192,512]{1,0:T(8,128)(2,1)S(1)}, u32[]{:S(2)}, u32[]{:S(2)}) collective-permute-start(bf16[192,512]{1,0:T(8,128)(2,1)S(1)} %level_0.4._.own_ref), channel_id=1, source_target_pairs={{0,64},{16,80},{32,96},{48,112},{64,0},{80,16},{96,32},{112,48},{1... | collective-permute-start | bytes 589832 | tf_op jit(solution)/shard_map/ppermute | solution.py:345
  29.4 23.0 %collective-permute-start.3 = (bf16[1040,512]{1,0:T(8,128)(2,1)S(1)}, bf16[1040,512]{1,0:T(8,128)(2,1)S(1)}, u32[]{:S(2)}, u32[]{:S(2)}) collective-permute-start(bf16[1040,512]{1,0:T(8,128)(2,1)S(1)} %get-tuple-element.23.own_ref), channel_id=1, source_target_pairs={{63,64},{127,128},{191,192},{255,256},{319,320},{383,384},{447,448... | collective-permute-start | bytes 3194888 | tf_op jit(solution)/shard_map/ppermute | solution.py:376
  40.1 13.2 %collective-permute-start.2 = (bf16[192,512]{1,0:T(8,128)(2,1)S(1)}, bf16[192,512]{1,0:T(8,128)(2,1)S(1)}, u32[]{:S(2)}, u32[]{:S(2)}) collective-permute-start(bf16[192,512]{1,0:T(8,128)(2,1)S(1)} %level_1.1.own_ref), channel_id=1, source_target_pairs={{0,2},{1,3},{2,0},{3,1},{4,6},{5,7},{6,4},{7,5},{8,10},{9,11},{10,... | collective-permute-start | bytes 589832 | tf_op jit(solution)/shard_map/ppermute | solution.py:345
